TPU v7x, 32 devices: a whole 2x2x4 slice. The times are simulated.
32 devices in a mesh: space: 2 (over y), tensor: 16 (over z, x, core).
Axes of the slice: x: 2, y: 2, z: 4, core: 2. Of those that a mesh axis runs over, the one named last changes fastest.
Arguments:
- tokens: bfloat16 [784, 6144], P('space', 'tensor'), may hold values from -6 to 6
- grad_out: bfloat16 [784, 6144], P('space', 'tensor'), may hold values from -6 to 6
- w_in: bfloat16 [6144, 12288], P(None, 'tensor'), may hold values from -0.078125 to 0.078125
- w_out: bfloat16 [12288, 6144], P('tensor'), may hold values from -0.0546875 to 0.0546875
- conv_kernel: float32 [9, 12288], P(None, 'tensor'), may hold values from -2 to 2
- conv_bias: float32 [12288], P('tensor'), may hold values from -3 to 3
Outputs:
- grad_tokens: bfloat16 [784, 6144], P('space', 'tensor')
- grad_w_in: bfloat16 [6144, 12288], P('space', 'tensor')
- grad_w_out: bfloat16 [12288, 6144], P('tensor', 'space')
- grad_kernel: float32 [9, 12288], P(None, 'tensor')
- grad_bias: float32 [12288], P('tensor')
All inputs are finite; a program needn't handle non-finite values.
Results may differ from a plain program's by a relative error of at most 0.014.
Values may be sent and summed in bfloat16 or wider, within the bound.
No kernel may reach another device: no remote copies, remote signals or barrier semaphores. Data moves between devices by JAX's collectives and lax.ppermute only.
A program may use at most 192 MiB of HBM per device.

v0:
```python
import jax
import jax.numpy as jnp
from jax import lax
from jax.sharding import PartitionSpec as P

GW = 56


OFFSETS = [(-1, -1), (-1, 0), (-1, 1), (0, -1), (0, 0), (0, 1), (1, -1), (1, 0), (1, 1)]


def padded_2(block, sides, width):
    for axis, dim in sides:
        count = lax.axis_size(axis)
        forward = [(i, i + 1) for i in range(count - 1)]
        backward = [(target, source) for source, target in forward]
        low = lax.ppermute(
            lax.slice_in_dim(block, block.shape[dim] - width, None, axis=dim), axis, forward
        )
        high = lax.ppermute(lax.slice_in_dim(block, 0, width, axis=dim), axis, backward)
        block = jnp.concatenate([low, block, high], axis=dim)
    return block


def gelu_parts(pre):
    inner = 0.7978845608 * (pre + 0.044715 * pre * pre * pre)
    tanh_val = jnp.tanh(inner)
    value = 0.5 * pre * (1.0 + tanh_val)
    slope = 0.5 * (1.0 + tanh_val) + 0.5 * pre * (1.0 - tanh_val * tanh_val) * 0.7978845608 * (
        1.0 + 3.0 * 0.044715 * pre * pre
    )
    return (value, slope)


def shards(tokens, grad_out, w_in, w_out, conv_kernel, conv_bias):
    tok_rows = tokens.shape[0]
    grid_rows = tok_rows // GW
    ff_local = w_in.shape[1]
    full_tokens, full_grad = (
        lax.all_gather(tokens, "tensor", axis=1, tiled=True),
        lax.all_gather(grad_out, "tensor", axis=1, tiled=True),
    )
    hidden_acc = jnp.dot(full_tokens, w_in, preferred_element_type=jnp.float32)
    grad_act = lax.dot_general(
        full_grad, w_out, (((1,), (1,)), ((), ())), preferred_element_type=jnp.float32
    )
    hidden = hidden_acc.astype(jnp.bfloat16).reshape(grid_rows, GW, ff_local)
    rimmed = padded_2(hidden, (("space", 0),), 1)
    padded = jnp.pad(rimmed, ((0, 0), (1, 1), (0, 0))).astype(jnp.float32)
    pre = jnp.zeros((grid_rows, GW, ff_local), jnp.float32) + conv_bias
    for index, (da, db) in enumerate(OFFSETS):
        pre = pre + conv_kernel[index] * padded[1 + da : 1 + da + grid_rows, 1 + db : 1 + db + GW]
    act, slope = gelu_parts(pre)
    act = act.astype(jnp.bfloat16).reshape(tok_rows, ff_local)
    grad_pre = (grad_act.reshape(grid_rows, GW, ff_local) * slope).astype(jnp.bfloat16)
    out_term = lax.dot_general(
        act, full_grad, (((0,), (0,)), ((), ())), preferred_element_type=jnp.float32
    )
    grad_f = grad_pre.astype(jnp.float32)
    kernel_rows = []
    for index, (da, db) in enumerate(OFFSETS):
        kernel_rows.append(
            jnp.sum(grad_f * padded[1 + da : 1 + da + grid_rows, 1 + db : 1 + db + GW], axis=(0, 1))
        )
    kernel_terms = jnp.stack(kernel_rows)
    bias_term = jnp.sum(grad_f, axis=(0, 1))
    grad_kernel, grad_bias = lax.psum((kernel_terms, bias_term), "space")
    grad_rimmed = padded_2(grad_pre, (("space", 0),), 1)
    grad_padded = jnp.pad(grad_rimmed, ((0, 0), (1, 1), (0, 0))).astype(jnp.float32)
    grad_hidden = jnp.zeros((grid_rows, GW, ff_local), jnp.float32)
    for index, (da, db) in enumerate(OFFSETS):
        grad_hidden = (
            grad_hidden
            + conv_kernel[index] * grad_padded[1 - da : 1 - da + grid_rows, 1 - db : 1 - db + GW]
        )
    grad_hidden = grad_hidden.astype(jnp.bfloat16).reshape(tok_rows, ff_local)
    in_term = lax.dot_general(
        full_tokens, grad_hidden, (((0,), (0,)), ((), ())), preferred_element_type=jnp.float32
    )
    summed_in, summed_out = (
        lax.psum_scatter(
            in_term.astype(jnp.bfloat16), "space", scatter_dimension=0, tiled=True
        ).astype(jnp.float32),
        lax.psum_scatter(
            out_term.astype(jnp.bfloat16), "space", scatter_dimension=1, tiled=True
        ).astype(jnp.float32),
    )
    grad_w_in = summed_in.astype(jnp.bfloat16)
    grad_w_out = summed_out.astype(jnp.bfloat16)
    token_terms = lax.dot_general(
        grad_hidden, w_in, (((1,), (1,)), ((), ())), preferred_element_type=jnp.float32
    )
    grad_tokens = lax.psum_scatter(
        token_terms.astype(jnp.bfloat16), "tensor", scatter_dimension=1, tiled=True
    )
    return (grad_tokens, grad_w_in, grad_w_out, grad_kernel, grad_bias)


def solution(mesh):
    return jax.shard_map(
        shards,
        mesh=mesh,
        in_specs=(
            P("space", "tensor"),
            P("space", "tensor"),
            P(None, "tensor"),
            P("tensor", None),
            P(None, "tensor"),
            P("tensor"),
        ),
        out_specs=(
            P("space", "tensor"),
            P("space", "tensor"),
            P("tensor", "space"),
            P(None, "tensor"),
            P("tensor"),
        ),
        check_vma=False,
    )
```

profile of v0, /device:TPU:0, one launch (start us, length us, event | category | flops | bytes accessed | tf_op | source)
XLA Modules:
  0.0 478.0 jit_solution(18130688776964309026)
XLA Ops:
  7.2 0.0 all-gather.5.cloned.1.call-start
  7.2 0.7 all-gather.5.cloned.1.call-update
  7.9 0.0 all-gather.3.cloned.1.call-start
  7.9 0.7 all-gather.3.cloned.1.call-update
  8.7 0.0 reduce-scatter.10.cloned.1.call-start
  8.7 1.1 slice_reduce_fusion.8
  9.8 59.7 %all-gather.5.cloned.1.call-done = bf16[392,6144]{1,0:T(8,128)(2,1)} async-done(((bf16[392,384]{1,0:T(8,128)(2,1)}), bf16[392,6144]{1,0:T(8,128)(2,1)}) %all-gather.5.cloned.1.call-update) | async-done | bytes 4816912 | tf_op jit(solution)/shard_map/all_gather | solution.py:40
  69.5 9.0 %convolution_convert_fusion.3 = bf16[392,768]{1,0:T(8,128)(2,1)S(1)} fusion(bf16[392,6144]{1,0:T(8,128)(2,1)} %all-gather.5.cloned.1.call-done, bf16[6144,768]{1,0:T(8,128)(2,1)} %param.8), kind=kOutput, calls=%fused_computation.19 | convolution fusion | flops 3699677184 | bytes 14856192 | tf_op jit(solution)/shard_map/dot_general | solution.py:43
  78.6 3.4 collective-permute-start
  82.0 1.3 collective-permute-start.1
  83.3 43.2 %all-gather.3.cloned.1.call-done = bf16[392,6144]{1,0:T(8,128)(2,1)} async-done(((bf16[392,384]{1,0:T(8,128)(2,1)}), bf16[392,6144]{1,0:T(8,128)(2,1)}) %all-gather.3.cloned.1.call-update) | async-done | bytes 4816912 | tf_op jit(solution)/shard_map/all_gather | solution.py:41
  126.5 8.2 %fusion.36 = f32[392,768]{1,0:T(8,128)S(1)} fusion(bf16[392,6144]{1,0:T(8,128)(2,1)} %all-gather.3.cloned.1.call-done, bf16[768,6144]{1,0:T(8,128)(2,1)} %param.9), kind=kOutput, calls=%fused_computation.77 | convolution fusion | flops 3699376128 | bytes 15458304 | tf_op jit(solution)/shard_map/dot_general | solution.py:44
  134.8 0.0 collective-permute-done
  134.8 0.0 collective-permute-done.1
  134.8 0.0 copy-start
  134.8 0.2 fusion.33
  135.0 0.4 copy-done
  135.5 0.0 slice-start
  135.5 0.0 slice-start.1
  135.5 3.1 fusion.17
  138.6 3.4 collective-permute-start.2
  142.0 1.3 collective-permute-start.3
  143.3 0.9 collective-permute-done.2
  144.1 4.2 collective-permute-done.3
  148.3 0.2 fusion.27
  148.6 0.0 slice-start.2
  148.6 0.9 fusion.19
  149.5 0.0 slice-done
  149.5 0.0 slice-done.1
  149.5 0.3 slice-done.2
  149.8 5.6 %convolution_convert_fusion.2 = bf16[392,6144]{1,0:T(8,128)(2,1)} fusion(bf16[392,768]{1,0:T(8,128)(2,1)S(1)} %bitcast.25, bf16[6144,768]{1,0:T(8,128)(2,1)S(1)} %bitcast.30), kind=kOutput, calls=%fused_computation.3 | convolution fusion | flops 3701784576 | bytes 14856192 | tf_op jit(solution)/shard_map/dot_general | solution.py:90
  155.4 8.0 %copy.13 = bf16[392,6144]{0,1:T(8,128)(2,1)} copy(bf16[392,6144]{1,0:T(8,128)(2,1)} %convolution_convert_fusion.2) | data formatting | bytes 9633792
  163.4 0.0 reduce-scatter.10.cloned.1.call-update
  163.4 0.2 reduce-scatter.6.cloned.1.call-start
  163.6 9.9 %fusion = bf16[6144,768]{0,1:T(8,128)(2,1)} fusion(bf16[392,768]{1,0:T(8,128)(2,1)S(1)} %bitcast.26, bf16[392,6144]{1,0:T(8,128)(2,1)} %all-gather.5.cloned.1.call-done), kind=kOutput, calls=%fused_computation.2 | convolution fusion | flops 3704094720 | bytes 14856192 | tf_op jit(solution)/shard_map/dot_general | solution.py:77
  173.5 0.0 reduce-scatter.6.cloned.1.call-update
  173.6 0.0 reduce-scatter.8.cloned.1.call-start
  173.6 0.4 multiply_convert_fusion
  174.0 10.3 %convolution_convert_fusion = bf16[768,6144]{1,0:T(8,128)(2,1)} fusion(bf16[392,768]{1,0:T(8,128)(2,1)S(1)} %bitcast.27, bf16[392,6144]{1,0:T(8,128)(2,1)} %all-gather.3.cloned.1.call-done), kind=kOutput, calls=%fused_computation | convolution fusion | flops 3704094720 | bytes 14856192 | tf_op jit(solution)/shard_map/dot_general | solution.py:56
  184.3 0.0 reduce-scatter.8.cloned.1.call-update
  184.4 0.1 stack.39
  184.5 7.8 %all-reduce.2 = (f32[9,768]{1,0:T(8,128)}, f32[768]{0:T(1024)}) all-reduce(f32[9,768]{1,0:T(8,128)S(1)} %stack.39, f32[768]{0:T(1024)S(1)} %get-tuple-element.24), channel_id=1, replica_groups=mesh['space'=2,'tensor'=16] {'space'}, use_global_device_ids=true, to_apply=%region_12.13 | all-reduce | flops 7680 | bytes 61440 | tf_op jit(solution)/shard_map/psum | solution.py:67
  192.3 53.8 %reduce-scatter.10.cloned.1.call-done = bf16[384,392]{1,0:T(8,128)(2,1)} async-done(((bf16[6144,392]{1,0:T(8,128)(2,1)}), bf16[384,392]{1,0:T(8,128)(2,1)}) %reduce-scatter.10.cloned.1.call-update) | async-done | bytes 301072
  246.1 1.9 copy.14
  247.9 110.1 %reduce-scatter.6.cloned.1.call-done = bf16[3072,768]{0,1:T(8,128)(2,1)} async-done(((bf16[6144,768]{0,1:T(8,128)(2,1)}), bf16[3072,768]{0,1:T(8,128)(2,1)}) %reduce-scatter.6.cloned.1.call-update) | async-done | bytes 4718608 | tf_op jit(solution)/shard_map/reduce_scatter | solution.py:81
  358.0 6.6 %copy.12 = bf16[3072,768]{1,0:T(8,128)(2,1)} copy(bf16[3072,768]{0,1:T(8,128)(2,1)} %reduce-scatter.6.cloned.1.call-done) | data formatting | bytes 9437184
  364.6 106.8 %reduce-scatter.8.cloned.1.call-done = bf16[768,3072]{1,0:T(8,128)(2,1)} async-done(((bf16[768,6144]{1,0:T(8,128)(2,1)}), bf16[768,3072]{1,0:T(8,128)(2,1)}) %reduce-scatter.8.cloned.1.call-update) | async-done | bytes 4718608 | tf_op jit(solution)/shard_map/reduce_scatter | solution.py:84
  (12 shorter events, 0.1 us)
Async XLA Ops:
  7.2 62.3 %all-gather.5.cloned.1.call-start = ((), (), s32[]{:S(2)}) async-start(), calls=%async_computation.4 | async-start | bytes 5117952 | tf_op jit(solution)/shard_map/all_gather | solution.py:40
  7.9 118.6 %all-gather.3.cloned.1.call-start = ((), (), s32[]{:S(2)}) async-start(), calls=%async_computation.3 | async-start | bytes 5117952 | tf_op jit(solution)/shard_map/all_gather | solution.py:41
  8.7 237.4 %reduce-scatter.10.cloned.1.call-start = ((), (), s32[]{:S(2)}) async-start(), calls=%async_computation.7 | async-start | bytes 6684672
  78.6 56.2 %collective-permute-start = (bf16[1,56,768]{2,1,0:T(8,128)(2,1)S(1)}, bf16[1,56,768]{2,1,0:T(8,128)(2,1)S(1)}, u32[]{:S(2)}, u32[]{:S(2)}) collective-permute-start(bf16[1,56,768]{2,1,0:T(8,128)(2,1)S(1)} %get-tuple-element.40), channel_id=1, source_target_pairs={{0,16},{1,17},{2,18},{3,19},{4,20},{5,21},{6,22},{7,23},{8,24},{9,... | collective-permute-start | bytes 258056 | tf_op jit(solution)/shard_map/ppermute | solution.py:17
  82.0 52.8 %collective-permute-start.1 = (bf16[1,56,768]{2,1,0:T(8,128)(2,1)S(1)}, bf16[1,56,768]{2,1,0:T(8,128)(2,1)S(1)}, u32[]{:S(2)}, u32[]{:S(2)}) collective-permute-start(bf16[1,56,768]{2,1,0:T(8,128)(2,1)S(1)} %get-tuple-element.41), channel_id=1, source_target_pairs={{16,0},{17,1},{18,2},{19,3},{20,4},{21,5},{22,6},{23,7},{24,8},{25... | collective-permute-start | bytes 258056 | tf_op jit(solution)/shard_map/ppermute | solution.py:20
  134.8 0.7 copy-start
  135.5 14.0 %slice-start = ((s8[9437184]{0:T(1024)(128)(4,1)}), s8[4194304]{0:T(1024)(128)(4,1)S(1)}, s32[]{:S(2)}) async-start(s8[9437184]{0:T(1024)(128)(4,1)} %bitcast.29), calls=%async_computation.8 | async-start | bytes 8388608
  135.5 14.0 %slice-start.1 = ((s8[9437184]{0:T(1024)(128)(4,1)}), s8[4194304]{0:T(1024)(128)(4,1)S(1)}, s32[]{:S(2)}) async-start(s8[9437184]{0:T(1024)(128)(4,1)} %bitcast.29), calls=%async_computation.9 | async-start | bytes 8388608
  138.6 5.6 %collective-permute-start.2 = (bf16[1,56,768]{2,1,0:T(8,128)(2,1)S(1)}, bf16[1,56,768]{2,1,0:T(8,128)(2,1)S(1)}, u32[]{:S(2)}, u32[]{:S(2)}) collective-permute-start(bf16[1,56,768]{2,1,0:T(8,128)(2,1)S(1)} %get-tuple-element.38), channel_id=1, source_target_pairs={{0,16},{1,17},{2,18},{3,19},{4,20},{5,21},{6,22},{7,23},{8,24},{9,... | collective-permute-start | bytes 258056 | tf_op jit(solution)/shard_map/ppermute | solution.py:17
  142.0 6.4 %collective-permute-start.3 = (bf16[1,56,768]{2,1,0:T(8,128)(2,1)S(1)}, bf16[1,56,768]{2,1,0:T(8,128)(2,1)S(1)}, u32[]{:S(2)}, u32[]{:S(2)}) collective-permute-start(bf16[1,56,768]{2,1,0:T(8,128)(2,1)S(1)} %get-tuple-element.39), channel_id=1, source_target_pairs={{16,0},{17,1},{18,2},{19,3},{20,4},{21,5},{22,6},{23,7},{24,8},{25... | collective-permute-start | bytes 258056 | tf_op jit(solution)/shard_map/ppermute | solution.py:20
  148.6 1.2 slice-start.2
  163.4 194.6 %reduce-scatter.6.cloned.1.call-start = ((), (), s32[]{:S(2)}) async-start(), calls=%async_computation.5 | async-start | bytes 14155776 | tf_op jit(solution)/shard_map/reduce_scatter | solution.py:81
  173.6 297.9 %reduce-scatter.8.cloned.1.call-start = ((), (), s32[]{:S(2)}) async-start(), calls=%async_computation.6 | async-start | bytes 14155776 | tf_op jit(solution)/shard_map/reduce_scatter | solution.py:84
Sparse Core Ops, SparseCore 0:
  10.2 59.3 all-gather.4
  71.7 54.7 all-gather.2
  163.5 82.4 reduce-scatter.9
  248.3 109.6 reduce-scatter.5
  360.9 110.5 reduce-scatter.7
where the time goes:
time: 479 us; the launch traced here: 478 us
  waiting for transfers between devices  380 us (79%)
  matrix products  43 us (9%)
  local copies, waits for them, and re-layouts  18.5 us (4%)
  between operations  14 us (3%)
  starting transfers between devices  9.73 us (2%)
  blocking collectives  7.82 us (2%)
  other arithmetic  4.79 us (1%)
    reduce_scatter x1, waiting for transfers between devices, shards(): lax.psum_scatter(in_term.astype(jnp.bfloat16), 'space', scatter_dimension...  110 us
    reduce_scatter x1, waiting for transfers between devices, shards(): lax.psum_scatter(out_term.astype(jnp.bfloat16), 'space', scatter_dimensio...  107 us
    all_gather x1, waiting for transfers between devices, shards(): lax.all_gather(tokens, 'tensor', axis=1, tiled=True)  59.7 us
    unnamed x6, waiting for transfers between devices  55.2 us
    all_gather x1, waiting for transfers between devices, shards(): lax.all_gather(grad_out, 'tensor', axis=1, tiled=True)  43.2 us
    unnamed x11, local copies, waits for them, and re-layouts  17.2 us
    dot_general x1, matrix products, shards(): lax.dot_general(act, full_grad, (((0,), (0,)), ((), ())), preferred_eleme...  10.3 us
    dot_general x1, matrix products, shards(): lax.dot_general(full_tokens, grad_hidden, (((0,), (0,)), ((), ())), prefe...  9.91 us
  transfers between devices with their start and end apart: 9, of which 7 were waited for; matrix products, arithmetic and copies ran while one was open for 10% of the time, Pallas kernels for 0%

commit v1 on v0

v1 whole, which is shorter than its diff:
```python
import jax
import jax.numpy as jnp
from jax import lax
from jax.experimental import pallas as pl
from jax.experimental.pallas import tpu as pltpu
from jax.sharding import PartitionSpec as P

GW = 56
NZ, NX, NC = 4, 2, 2

OFFSETS = [(-1, -1), (-1, 0), (-1, 1), (0, -1), (0, 0), (0, 1), (1, -1), (1, 0), (1, 1)]

BF = jnp.bfloat16
F32 = jnp.float32


def gelu_parts(pre):
    inner = 0.7978845608 * (pre + 0.044715 * pre * pre * pre)
    tanh_val = jnp.tanh(inner)
    value = 0.5 * pre * (1.0 + tanh_val)
    slope = 0.5 * (1.0 + tanh_val) + 0.5 * pre * (1.0 - tanh_val * tanh_val) * 0.7978845608 * (
        1.0 + 3.0 * 0.044715 * pre * pre
    )
    return (value, slope)


def padded_2(block, sides, width):
    for axis, dim in sides:
        count = lax.axis_size(axis)
        forward = [(i, i + 1) for i in range(count - 1)]
        backward = [(target, source) for source, target in forward]
        low = lax.ppermute(
            lax.slice_in_dim(block, block.shape[dim] - width, None, axis=dim), axis, forward
        )
        high = lax.ppermute(lax.slice_in_dim(block, 0, width, axis=dim), axis, backward)
        block = jnp.concatenate([low, block, high], axis=dim)
    return block


def shards_any(tokens, grad_out, w_in, w_out, conv_kernel, conv_bias):
    tok_rows = tokens.shape[0]
    grid_rows = tok_rows // GW
    ff_local = w_in.shape[1]
    full_tokens, full_grad = (
        lax.all_gather(tokens, "tensor", axis=1, tiled=True),
        lax.all_gather(grad_out, "tensor", axis=1, tiled=True),
    )
    hidden_acc = jnp.dot(full_tokens, w_in, preferred_element_type=F32)
    grad_act = lax.dot_general(full_grad, w_out, (((1,), (1,)), ((), ())), preferred_element_type=F32)
    hidden = hidden_acc.astype(BF).reshape(grid_rows, GW, ff_local)
    rimmed = padded_2(hidden, (("space", 0),), 1)
    padded = jnp.pad(rimmed, ((0, 0), (1, 1), (0, 0))).astype(F32)
    pre = jnp.zeros((grid_rows, GW, ff_local), F32) + conv_bias
    for index, (da, db) in enumerate(OFFSETS):
        pre = pre + conv_kernel[index] * padded[1 + da : 1 + da + grid_rows, 1 + db : 1 + db + GW]
    act, slope = gelu_parts(pre)
    act = act.astype(BF).reshape(tok_rows, ff_local)
    grad_pre = (grad_act.reshape(grid_rows, GW, ff_local) * slope).astype(BF)
    out_term = lax.dot_general(act, full_grad, (((0,), (0,)), ((), ())), preferred_element_type=F32)
    grad_f = grad_pre.astype(F32)
    kernel_rows = []
    for index, (da, db) in enumerate(OFFSETS):
        kernel_rows.append(
            jnp.sum(grad_f * padded[1 + da : 1 + da + grid_rows, 1 + db : 1 + db + GW], axis=(0, 1))
        )
    kernel_terms = jnp.stack(kernel_rows)
    bias_term = jnp.sum(grad_f, axis=(0, 1))
    grad_kernel, grad_bias = lax.psum((kernel_terms, bias_term), "space")
    grad_rimmed = padded_2(grad_pre, (("space", 0),), 1)
    grad_padded = jnp.pad(grad_rimmed, ((0, 0), (1, 1), (0, 0))).astype(F32)
    grad_hidden = jnp.zeros((grid_rows, GW, ff_local), F32)
    for index, (da, db) in enumerate(OFFSETS):
        grad_hidden = (
            grad_hidden
            + conv_kernel[index] * grad_padded[1 - da : 1 - da + grid_rows, 1 - db : 1 - db + GW]
        )
    grad_hidden = grad_hidden.astype(BF).reshape(tok_rows, ff_local)
    in_term = lax.dot_general(full_tokens, grad_hidden, (((0,), (0,)), ((), ())), preferred_element_type=F32)
    grad_w_in = lax.psum_scatter(in_term.astype(BF), "space", scatter_dimension=0, tiled=True)
    grad_w_out = lax.psum_scatter(out_term.astype(BF), "space", scatter_dimension=1, tiled=True)
    token_terms = lax.dot_general(grad_hidden, w_in, (((1,), (1,)), ((), ())), preferred_element_type=F32)
    grad_tokens = lax.psum_scatter(token_terms.astype(BF), "tensor", scatter_dimension=1, tiled=True)
    return (grad_tokens, grad_w_in, grad_w_out, grad_kernel, grad_bias)


def dev(z, x, c):
    return (z * NX + x) * NC + c


ALL = [(z, x, c) for z in range(NZ) for x in range(NX) for c in range(NC)]


def go_z(v, k=1):
    return lax.ppermute(v, "tensor", [(dev(z, x, c), dev((z + k) % NZ, x, c)) for z, x, c in ALL])


def go_x(v):
    return lax.ppermute(v, "tensor", [(dev(z, x, c), dev(z, 1 - x, c)) for z, x, c in ALL])


def go_c(v):
    return lax.ppermute(v, "tensor", [(dev(z, x, c), dev(z, x, 1 - c)) for z, x, c in ALL])


def go_y(v):
    return lax.ppermute(v, "space", [(0, 1), (1, 0)])


PARAMS = dict(vmem_limit_bytes=48 * 1024 * 1024)
NN = (((1,), (0,)), ((), ()))
NT = (((1,), (1,)), ((), ()))
TN = (((0,), (0,)), ((), ()))


def project(blocks, where_own, where_sib, w_own, w_sib, acc, out_dims):
    n = len(blocks)
    rows, bw = blocks[0].shape
    wide = out_dims is NN
    ff = w_own.shape[1] if wide else w_own.shape[0]
    index = jnp.stack(list(where_own) + list(where_sib)).astype(jnp.int32)

    def body(index_ref, *refs):
        bs, (wo, ws) = refs[:n], refs[n : n + 2]
        accs = refs[n + 2 : n + 4] if acc is not None else None
        oo, os = refs[-2:]
        i = pl.program_id(0)

        @pl.when(i == 0)
        def _():
            if accs is None:
                oo[...] = jnp.zeros_like(oo)
                os[...] = jnp.zeros_like(os)
            else:
                oo[...] = accs[0][...]
                os[...] = accs[1][...]

        for k in range(n):

            @pl.when(i == k)
            def _(k=k):
                b = bs[k][...]
                os[...] += lax.dot_general(b, ws[...], out_dims, preferred_element_type=F32)
                oo[...] += lax.dot_general(b, wo[...], out_dims, preferred_element_type=F32)

    whole = lambda i, r: (0, 0)
    if wide:
        w_specs = [
            pl.BlockSpec((bw, ff), lambda i, r: (r[i], 0)),
            pl.BlockSpec((bw, ff), lambda i, r: (r[n + i], 0)),
        ]
    else:
        w_specs = [
            pl.BlockSpec((ff, bw), lambda i, r: (0, r[i])),
            pl.BlockSpec((ff, bw), lambda i, r: (0, r[n + i])),
        ]
    extra = [] if acc is None else [pl.BlockSpec((rows, ff), whole)] * 2
    return pl.pallas_call(
        body,
        grid_spec=pltpu.PrefetchScalarGridSpec(
            num_scalar_prefetch=1,
            grid=(n,),
            in_specs=[pl.BlockSpec((rows, bw), whole)] * n + w_specs + extra,
            out_specs=[pl.BlockSpec((rows, ff), whole)] * 2,
        ),
        out_shape=[jax.ShapeDtypeStruct((rows, ff), F32)] * 2,
        compiler_params=pltpu.CompilerParams(**PARAMS),
        cost_estimate=pl.CostEstimate(
            flops=4 * n * rows * bw * ff, transcendentals=0, bytes_accessed=4 * n * bw * ff + 16 * rows * ff
        ),
        name="project",
    )(index, *blocks, w_own, w_sib, *(acc or ()))


def token_grads(gh_own, gh_sib, w_own, w_sib, where_own, where_sib, bw):
    n = len(where_own)
    rows, ff = gh_own.shape
    index = jnp.stack(list(where_own) + list(where_sib)).astype(jnp.int32)

    def body(index_ref, go, gs, wo, ws, *outs):
        i = pl.program_id(0)
        t = lax.dot_general(go[...], wo[...], NT, preferred_element_type=F32)
        t = t + lax.dot_general(gs[...], ws[...], NT, preferred_element_type=F32)
        for k in range(n):

            @pl.when(i == k)
            def _(k=k):
                outs[k][...] = t.astype(BF)

    whole = lambda i, r: (0, 0)
    return pl.pallas_call(
        body,
        grid_spec=pltpu.PrefetchScalarGridSpec(
            num_scalar_prefetch=1,
            grid=(n,),
            in_specs=[
                pl.BlockSpec((rows, ff), whole),
                pl.BlockSpec((rows, ff), whole),
                pl.BlockSpec((bw, ff), lambda i, r: (r[i], 0)),
                pl.BlockSpec((bw, ff), lambda i, r: (r[n + i], 0)),
            ],
            out_specs=[pl.BlockSpec((rows, bw), whole)] * n,
        ),
        out_shape=[jax.ShapeDtypeStruct((rows, bw), BF)] * n,
        compiler_params=pltpu.CompilerParams(**PARAMS),
        cost_estimate=pl.CostEstimate(
            flops=4 * n * rows * bw * ff, transcendentals=0, bytes_accessed=4 * n * bw * ff + 2 * n * rows * bw
        ),
        name="token_grads",
    )(index, gh_own, gh_sib, w_own, w_sib)


def weight_grad(core, own, sib, left, right, by_rows):
    _, n, rows, bw = own.shape
    ff = left.shape[1]

    def body(core_ref, o, s, l, r, out):
        cc = pl.program_id(1)

        def terms(src):
            if by_rows:
                t = lax.dot_general(src[0, 0], l[...], TN, preferred_element_type=F32)
                return t + lax.dot_general(src[1, 0], r[...], TN, preferred_element_type=F32)
            t = lax.dot_general(l[...], src[0, 0], TN, preferred_element_type=F32)
            return t + lax.dot_general(r[...], src[1, 0], TN, preferred_element_type=F32)

        @pl.when(cc == 0)
        def _():
            out[...] = terms(o).astype(BF)

        @pl.when(cc == 1)
        def _():
            out[...] = terms(s).astype(BF)

    place = lambda i, k, r: 2 * i + r[0] * (1 - k) + (1 - r[0]) * k
    if by_rows:
        out_spec = pl.BlockSpec((bw, ff), lambda i, k, r: (place(i, k, r), 0))
        shape = (2 * n * bw, ff)
    else:
        out_spec = pl.BlockSpec((ff, bw), lambda i, k, r: (0, place(i, k, r)))
        shape = (ff, 2 * n * bw)
    piece = pl.BlockSpec((2, 1, rows, bw), lambda i, k, r: (0, i, 0, 0))
    whole = pl.BlockSpec((rows, ff), lambda i, k, r: (0, 0))
    return pl.pallas_call(
        body,
        grid_spec=pltpu.PrefetchScalarGridSpec(
            num_scalar_prefetch=1, grid=(n, 2), in_specs=[piece, piece, whole, whole], out_specs=out_spec
        ),
        out_shape=jax.ShapeDtypeStruct(shape, BF),
        compiler_params=pltpu.CompilerParams(**PARAMS),
        cost_estimate=pl.CostEstimate(
            flops=8 * n * rows * bw * ff, transcendentals=0, bytes_accessed=12 * n * rows * bw + 4 * n * bw * ff
        ),
        name="weight_grad",
    )(core.reshape(1).astype(jnp.int32), own, sib, left, right)


def rims(block, recv, first_band):
    zero = jnp.zeros_like(recv)
    low = jnp.where(first_band, zero, recv)
    high = jnp.where(first_band, recv, zero)
    return jnp.concatenate([low, block, high], axis=0)


def shards(tokens, grad_out, w_in, w_out, conv_kernel, conv_bias):
    rows, bw = tokens.shape
    grid_rows = rows // GW
    ff = w_in.shape[1]
    s = lax.axis_index("space")
    t = lax.axis_index("tensor")
    z, x, c = t // (NX * NC), (t // NC) % NX, t % NC
    first = s == 0
    bar = lax.optimization_barrier

    send_in = lax.dynamic_index_in_dim(w_in.reshape(NZ * NX, NC, bw, ff), 1 - c, 1, keepdims=False)
    w_in_sib = go_c(send_in.reshape(NZ * NX * bw, ff))
    send_out = lax.dynamic_index_in_dim(w_out.reshape(ff, NZ * NX, NC, bw), 1 - c, 2, keepdims=False)
    w_out_sib = go_c(send_out.reshape(ff, NZ * NX * bw))

    def sib_at(zz, xx):
        return zz * NX + xx

    def own_at(zz, xx):
        return (zz * NX + xx) * NC + c

    zs = [(z - j) % NZ for j in range(NZ)]

    ta, tx = [tokens], []
    a1, x0 = go_z(tokens), go_x(tokens)
    a1, x0 = bar((a1, x0))
    a2, x1 = go_z(a1), go_x(a1)
    a2, x1 = bar((a2, x1))
    a3, x2 = go_z(a2), go_x(a2)
    a3, x2, g0 = bar((a3, x2, grad_out))
    ta, tx = [tokens, a1, a2, a3], [x0, x1, x2]
    b1, x3 = go_z(g0), go_x(a3)
    tx.append(x3)
    b1, x3, g0 = bar((b1, x3, g0))
    b2, y0 = go_z(b1), go_x(g0)
    b2, y0 = bar((b2, y0))
    b3, y1 = go_z(b2), go_x(b1)
    b3, y1 = bar((b3, y1))
    y3, y2 = go_x(b3), go_z(y1)
    ga, gx = [g0, b1, b2, b3], [y0, y1, y2, y3]

    def both(js, a, b):
        blocks = [a[j] for j in js] + [b[j] for j in js]
        own = [own_at(zs[j], x) for j in js] + [own_at(zs[j], 1 - x) for j in js]
        sib = [sib_at(zs[j], x) for j in js] + [sib_at(zs[j], 1 - x) for j in js]
        return blocks, own, sib

    part_own, part_sib = project(*both(range(NZ), ta, tx), w_in, w_in_sib, None, NN)
    hidden = (part_own + go_c(part_sib)).astype(BF).reshape(grid_rows, GW, ff)
    edge = jnp.where(first, hidden[grid_rows - 1 :], hidden[:1])
    rimmed = rims(hidden, go_y(edge), first)
    padded = jnp.pad(rimmed, ((0, 0), (1, 1), (0, 0))).astype(F32)
    pre = jnp.zeros((grid_rows, GW, ff), F32) + conv_bias
    for index, (da, db) in enumerate(OFFSETS):
        pre = pre + conv_kernel[index] * padded[1 + da : 1 + da + grid_rows, 1 + db : 1 + db + GW]
    act, slope = gelu_parts(pre)
    act = act.astype(BF).reshape(rows, ff)
    act_other = go_y(act)

    acc = project(*both((0, 1), ga, gx), w_out, w_out_sib, None, NT)
    part_own, part_sib = project(*both((2, 3), ga, gx), w_out, w_out_sib, acc, NT)
    grad_act = part_own + go_c(part_sib)
    grad_pre = (grad_act.reshape(grid_rows, GW, ff) * slope).astype(BF)
    edge = jnp.where(first, grad_pre[grid_rows - 1 :], grad_pre[:1])
    grad_rimmed = rims(grad_pre, go_y(edge), first)
    grad_padded = jnp.pad(grad_rimmed, ((0, 0), (1, 1), (0, 0))).astype(F32)
    grad_hidden = jnp.zeros((grid_rows, GW, ff), F32)
    for index, (da, db) in enumerate(OFFSETS):
        grad_hidden = (
            grad_hidden
            + conv_kernel[index] * grad_padded[1 - da : 1 - da + grid_rows, 1 - db : 1 - db + GW]
        )
    grad_hidden = grad_hidden.astype(BF).reshape(rows, ff)
    gh_sib = go_c(grad_hidden)
    gh_other = go_y(grad_hidden)

    order = [2, 1, 3, 0]
    zd = [(z + j) % NZ for j in order]
    away = token_grads(
        grad_hidden, gh_sib, w_in, w_in_sib,
        [own_at(q, 1 - x) for q in zd], [sib_at(q, 1 - x) for q in zd], bw,
    )
    came = [go_x(v) for v in away]
    home = token_grads(
        grad_hidden, gh_sib, w_in, w_in_sib,
        [own_at(q, x) for q in zd], [sib_at(q, x) for q in zd], bw,
    )
    sums = [a.astype(F32) + b.astype(F32) for a, b in zip(home, came)]
    total = sums[3]
    for k in range(3):
        total = total + go_z(sums[k].astype(BF), order[k]).astype(F32)
    grad_tokens = total.astype(BF)

    grad_f = grad_pre.astype(F32)
    terms = []
    for index, (da, db) in enumerate(OFFSETS):
        terms.append(
            jnp.sum(grad_f * padded[1 + da : 1 + da + grid_rows, 1 + db : 1 + db + GW], axis=(0, 1))
        )
    terms = jnp.stack(terms + [jnp.sum(grad_f, axis=(0, 1))])
    terms = terms + go_y(terms)
    grad_kernel, grad_bias = terms[:9], terms[9]

    def halves(a, b):
        stack = jnp.stack([v for pair in zip(a, b) for v in pair])

        def half(h):
            picks = []
            for l in range(NZ // 2):
                j = (z - (h * (NZ // 2) + l)) % NZ
                for xx in range(NX):
                    picks.append(lax.dynamic_index_in_dim(stack, j * NX + (xx ^ x), 0))
            return jnp.concatenate(picks, axis=0)

        mine = jnp.stack([half(s), go_y(half(1 - s))])
        return mine, go_c(mine)

    grad_w_out = weight_grad(c, *halves(ga, gx), act, act_other, False)
    grad_w_in = weight_grad(c, *halves(ta, tx), grad_hidden, gh_other, True)
    return (grad_tokens, grad_w_in, grad_w_out, grad_kernel, grad_bias)


def solution(mesh):
    split = mesh.shape["space"] == 2 and mesh.shape["tensor"] == NZ * NX * NC
    return jax.shard_map(
        shards if split else shards_any,
        mesh=mesh,
        in_specs=(
            P("space", "tensor"),
            P("space", "tensor"),
            P(None, "tensor"),
            P("tensor", None),
            P(None, "tensor"),
            P("tensor"),
        ),
        out_specs=(
            P("space", "tensor"),
            P("space", "tensor"),
            P("tensor", "space"),
            P(None, "tensor"),
            P("tensor"),
        ),
        check_vma=False,
    )
```

time: 479 us -> 282 us (0.59)
  waiting for transfers between devices: 380 us -> 121 us
  Pallas kernels: 0 us -> 55.8 us
  matrix products: 43 us -> 0 us
  local copies, waits for them, and re-layouts: 18.5 us -> 60.6 us
  starting transfers between devices: 9.73 us -> 31.8 us
  between operations: 14 us -> 1.23 us
  blocking collectives: 7.82 us -> 0 us
  other arithmetic: 4.79 us -> 10.5 us
    reduce_scatter x2 -> x0, waiting for transfers between devices: 217 us -> none  [the longest x1 110 us: shards(): lax.psum_scatter(in_term.astype(jnp.bfloat16), 'space', scatter_dimension...]
    ppermute x4 -> x35, waiting for transfers between devices: 5.08 us -> 121 us  [the longest x7 53.8 us: go_y(): return lax.ppermute(v, 'space', [(0, 1), (1, 0)])]
    all_gather x2 -> x0, waiting for transfers between devices: 103 us -> none  [the longest x1 59.7 us: shards(): lax.all_gather(tokens, 'tensor', axis=1, tiled=True)]
    pallas_call x0 -> x7, Pallas kernels: none -> 55.8 us  [the longest x2 22.5 us: weight_grad(): pl.pallas_call(body, grid_spec=pltpu.PrefetchScalarGridSpec(num_scalar_pr...]
    unnamed x6 -> x0, waiting for transfers between devices: 55.2 us -> none
    dot_general x5 -> x0, matrix products: 43 us -> none  [the longest x1 10.3 us: shards(): lax.dot_general(act, full_grad, (((0,), (0,)), ((), ())), preferred_eleme...]
    dynamic_slice x0 -> x4, local copies, waits for them, and re-layouts: none -> 37.2 us  [the longest x1 31.8 us: shards(): lax.dynamic_index_in_dim(w_out.reshape(ff, NZ * NX, NC, bw), 1 - c, 2, ke...]
    ppermute x4 -> x35, starting transfers between devices: 9.35 us -> 31.8 us  [the longest x11 12.6 us: go_x(): lax.ppermute(v, 'tensor', [(dev(z, x, c), dev(z, 1 - x, c)) for z, x, c i...]
  transfers between devices with their start and end apart: 9 -> 35, of which waited for: 7 -> 16; matrix products, arithmetic and copies ran while one was open for 10% -> 23% of each run, Pallas kernels for 0% -> 20%
where the time goes in v1:
time: 282 us; the launch traced here: 281 us
  waiting for transfers between devices  121 us (43%)
  local copies, waits for them, and re-layouts  60.6 us (21%)
  Pallas kernels  55.8 us (20%)
  starting transfers between devices  31.8 us (11%)
  other arithmetic  10.5 us (4%)
    ppermute x7, waiting for transfers between devices, go_y(): return lax.ppermute(v, 'space', [(0, 1), (1, 0)])  53.8 us
    ppermute x10, waiting for transfers between devices, go_z(): lax.ppermute(v, 'tensor', [(dev(z, x, c), dev((z + k) % NZ, x, c)) for z,...  53.3 us
    dynamic_slice x1, local copies, waits for them, and re-layouts, shards(): lax.dynamic_index_in_dim(w_out.reshape(ff, NZ * NX, NC, bw), 1 - c, 2, ke...  31.8 us
    pallas_call x2, Pallas kernels, weight_grad(): pl.pallas_call(body, grid_spec=pltpu.PrefetchScalarGridSpec(num_scalar_pr...  22.5 us
    pallas_call x3, Pallas kernels, project(): pl.pallas_call(body, grid_spec=pltpu.PrefetchScalarGridSpec(num_scalar_pr...  21.8 us
    reshape x1, local copies, waits for them, and re-layouts, shards(): w_out.reshape(ff, NZ * NX, NC, bw)  15.2 us
    ppermute x11, waiting for transfers between devices, go_x(): lax.ppermute(v, 'tensor', [(dev(z, x, c), dev(z, 1 - x, c)) for z, x, c i...  14.2 us
    ppermute x11, starting transfers between devices, go_x(): lax.ppermute(v, 'tensor', [(dev(z, x, c), dev(z, 1 - x, c)) for z, x, c i...  12.6 us
  transfers between devices with their start and end apart: 35, of which 16 were waited for; matrix products, arithmetic and copies ran while one was open for 23% of the time, Pallas kernels for 20%

profile of v1, /device:TPU:0, one launch (start us, length us, event | category | flops | bytes accessed | tf_op | source)
XLA Modules:
  0.0 281.2 jit_solution(3609096476585087789)
XLA Ops:
  0.6 4.8 %constant_dynamic-slice_fusion.16 = bf16[8,1,384,768]{3,2,1,0:T(8,128)(2,1)} fusion(bf16[8,2,384,768]{3,2,1,0:T(8,128)(2,1)} %bitcast.87, s32[]{:T(128)S(6)} %select_n.155), kind=kLoop, calls=%fused_computation.111 | loop fusion | bytes 9437188 | tf_op jit(solution)/shard_map/jit(dynamic_index_in_dim)/dynamic_slice | solution.py:274
  5.9 15.2 %reshape.53 = bf16[768,8,2,384]{3,2,1,0:T(2,128)(2,1)} reshape(bf16[768,6144]{1,0:T(8,128)(2,1)} %refs_4_.3) | data formatting | bytes 18874368 | tf_op jit(solution)/shard_map/reshape | solution.py:276
  21.2 31.8 %dynamic-slice_reduce_fusion = bf16[768,8,384]{2,1,0:T(8,128)(2,1)} fusion(bf16[768,8,2,384]{3,2,1,0:T(2,128)(2,1)} %reshape.53, s32[]{:T(128)S(6)} %select_n.155), kind=kLoop, calls=%fused_computation | loop fusion | bytes 9437188 | tf_op jit(solution)/shard_map/jit(dynamic_index_in_dim)/dynamic_slice | solution.py:276
  53.0 5.7 %copy.15 = bf16[96,8,8,384]{3,1,2,0:T(8,128)(2,1)} copy(bf16[96,8,8,384]{3,2,1,0:T(8,128)(2,1)} %bitcast.88) | data formatting | bytes 9437184
  58.7 3.0 %collective-permute-start = (bf16[392,384]{1,0:T(8,128)(2,1)S(1)}, bf16[392,384]{1,0:T(8,128)(2,1)S(1)}, u32[]{:S(2)}, u32[]{:S(2)}) collective-permute-start(bf16[392,384]{1,0:T(8,128)(2,1)S(1)} %copy-done.1), channel_id=1, source_target_pairs={{0,4},{1,5},{2,6},{3,7},{4,8},{5,9},{6,10},{7,11},{8,12},{9,13},{1... | collective-permute-start | bytes 903176 | tf_op jit(solution)/shard_map/ppermute | solution.py:94
  61.8 1.5 collective-permute-start.1
  63.8 7.3 %collective-permute-done.refs_1_ = bf16[392,384]{1,0:T(8,128)(2,1)S(1)} collective-permute-done((bf16[392,384]{1,0:T(8,128)(2,1)S(1)}, bf16[392,384]{1,0:T(8,128)(2,1)S(1)}, u32[]{:S(2)}, u32[]{:S(2)}) %collective-permute-start) | collective-permute-done | bytes 301088 | tf_op jit(solution)/shard_map/ppermute | solution.py:94
  71.1 1.0 collective-permute-start.2
  72.1 1.5 collective-permute-start.3
  73.7 7.7 %collective-permute-done.2.refs_2_ = bf16[392,384]{1,0:T(8,128)(2,1)S(1)} collective-permute-done((bf16[392,384]{1,0:T(8,128)(2,1)S(1)}, bf16[392,384]{1,0:T(8,128)(2,1)S(1)}, u32[]{:S(2)}, u32[]{:S(2)}) %collective-permute-start.2) | collective-permute-done | bytes 301088 | tf_op jit(solution)/shard_map/ppermute | solution.py:94
  81.4 1.4 collective-permute-start.5
  82.9 7.9 %collective-permute-done.4.refs_3_ = bf16[392,384]{1,0:T(8,128)(2,1)S(1)} collective-permute-done((bf16[392,384]{1,0:T(8,128)(2,1)S(1)}, bf16[392,384]{1,0:T(8,128)(2,1)S(1)}, u32[]{:S(2)}, u32[]{:S(2)}) %collective-permute-start.4) | collective-permute-done | bytes 301088 | tf_op jit(solution)/shard_map/ppermute | solution.py:94
  90.8 1.0 collective-permute-start.7
  91.9 5.7 %collective-permute-done.7.refs_7_ = bf16[392,384]{1,0:T(8,128)(2,1)S(1)} collective-permute-done((bf16[392,384]{1,0:T(8,128)(2,1)S(1)}, bf16[392,384]{1,0:T(8,128)(2,1)S(1)}, u32[]{:S(2)}, u32[]{:S(2)}) %collective-permute-start.7) | collective-permute-done | bytes 301088 | tf_op jit(solution)/shard_map/ppermute | solution.py:98
  97.6 2.8 collective-permute-done.6.refs_1_
  100.4 1.0 collective-permute-start.11
  101.4 1.0 collective-permute-start.9
  102.5 6.5 %collective-permute-done.8.refs_0_ = bf16[392,384]{1,0:T(8,128)(2,1)S(1)} collective-permute-done((bf16[392,384]{1,0:T(8,128)(2,1)S(1)}, bf16[392,384]{1,0:T(8,128)(2,1)S(1)}, u32[]{:S(2)}, u32[]{:S(2)}) %collective-permute-start.8) | collective-permute-done | bytes 301088 | tf_op jit(solution)/shard_map/ppermute | solution.py:94
  109.0 2.9 %collective-permute-done.9.refs_2_ = bf16[392,384]{1,0:T(8,128)(2,1)S(1)} collective-permute-done((bf16[392,384]{1,0:T(8,128)(2,1)S(1)}, bf16[392,384]{1,0:T(8,128)(2,1)S(1)}, u32[]{:S(2)}, u32[]{:S(2)}) %collective-permute-start.9) | collective-permute-done | bytes 301088 | tf_op jit(solution)/shard_map/ppermute | solution.py:98
  112.0 10.1 %collective-permute-done.10.refs_1_ = bf16[392,384]{1,0:T(8,128)(2,1)S(1)} collective-permute-done((bf16[392,384]{1,0:T(8,128)(2,1)S(1)}, bf16[392,384]{1,0:T(8,128)(2,1)S(1)}, u32[]{:S(2)}, u32[]{:S(2)}) %collective-permute-start.10) | collective-permute-done | bytes 301088 | tf_op jit(solution)/shard_map/ppermute | solution.py:94
  122.1 1.0 collective-permute-start.13
  123.2 7.4 %collective-permute-done.12.refs_2_ = bf16[392,384]{1,0:T(8,128)(2,1)S(1)} collective-permute-done((bf16[392,384]{1,0:T(8,128)(2,1)S(1)}, bf16[392,384]{1,0:T(8,128)(2,1)S(1)}, u32[]{:S(2)}, u32[]{:S(2)}) %collective-permute-start.12) | collective-permute-done | bytes 301088 | tf_op jit(solution)/shard_map/ppermute | solution.py:94
  130.9 10.0 %project.5 = (f32[392,768]{1,0:T(8,128)S(1)}, f32[392,768]{1,0:T(8,128)S(1)}) custom-call(s32[16]{0:T(128)S(1)} %stack.249.index_ref, bf16[392,384]{1,0:T(8,128)(2,1)S(1)} %copy-done.1, bf16[392,384]{1,0:T(8,128)(2,1)S(1)} %collective-permute-done.refs_1_, bf16[392,384]{1,0:T(8,128)(2,1)S(1)} %collective-permute-done.2.refs_2_, ...), custom_call_target="tpu_custom_call" | custom-call | flops 3699376128 | bytes 14254080 | tf_op jit(solution)/shard_map/project/pallas_call | solution.py:157
  141.4 1.6 collective-permute-start.31
  143.0 5.8 %project.3 = (f32[392,768]{1,0:T(8,128)S(1)}, f32[392,768]{1,0:T(8,128)S(1)}) custom-call(s32[8]{0:T(128)S(1)} %stack.248.index_ref, bf16[392,384]{1,0:T(8,128)(2,1)S(1)} %copy-done, bf16[392,384]{1,0:T(8,128)(2,1)S(1)} %collective-permute-done.6.refs_1_, bf16[392,384]{1,0:T(8,128)(2,1)S(1)} %collective-permute-done.9.refs_2_, ...), custom_call_target="tpu_custom_call" | custom-call | flops 1849688064 | bytes 9535488 | tf_op jit(solution)/shard_map/project/pallas_call | solution.py:157
  148.8 6.0 %project.4 = (f32[392,768]{1,0:T(8,128)S(1)}, f32[392,768]{1,0:T(8,128)S(1)}) custom-call(s32[8]{0:T(128)S(1)} %stack.241.index_ref, bf16[392,384]{1,0:T(8,128)(2,1)S(1)} %collective-permute-done.8.refs_0_, bf16[392,384]{1,0:T(8,128)(2,1)S(1)} %collective-permute-done.10.refs_1_, bf16[392,384]{1,0:T(8,128)(2,1)S(1)} %collective-permute-done.12.refs_2_, ...), custom_call_target="tpu_custom_call" | custom-call | flops 1849688064 | bytes 9535488 | tf_op jit(solution)/shard_map/project/pallas_call | solution.py:157
  156.7 1.6 collective-permute-start.18
  158.3 12.5 %collective-permute-done.31 = bf16[4,392,384]{2,1,0:T(8,128)(2,1)S(1)} collective-permute-done((bf16[4,392,384]{2,1,0:T(8,128)(2,1)S(1)}, bf16[4,392,384]{2,1,0:T(8,128)(2,1)S(1)}, u32[]{:S(2)}, u32[]{:S(2)}) %collective-permute-start.31) | collective-permute-done | bytes 1204256 | tf_op jit(solution)/shard_map/ppermute | solution.py:106
  170.8 1.7 pad_maximum_fusion.1.o
  172.6 25.4 %collective-permute-done.18 = bf16[1,56,768]{2,1,0:T(8,128)(2,1)S(1)} collective-permute-done((bf16[1,56,768]{2,1,0:T(8,128)(2,1)S(1)}, bf16[1,56,768]{2,1,0:T(8,128)(2,1)S(1)}, u32[]{:S(2)}, u32[]{:S(2)}) %collective-permute-start.18) | collective-permute-done | bytes 86048 | tf_op jit(solution)/shard_map/ppermute | solution.py:106
  198.8 3.1 %fusion.16 = (f32[768]{0:T(1024)S(1)}, f32[768]{0:T(1024)S(1)}, f32[768]{0:T(1024)S(1)}, f32[768]{0:T(1024)S(1)}, f32[768]{0:T(1024)S(1)}, /*index=5*/f32[768]{0...) fusion(f32[9,58,768]{2,1,0:T(8,128)S(1)} %fusion.32, ...), kind=kLoop, calls=%fused_computation.33 | loop fusion | flops 17152512 | bytes 13910016 | tf_op jit(solution)/shard_map/reduce_sum | solution.py:361
  201.9 1.6 collective-permute-start.19
  203.5 1.7 pad_maximum_fusion.o
  205.2 1.3 collective-permute-done.19
  208.0 1.6 collective-permute-start.33
  210.5 14.6 %collective-permute-done.34 = f32[10,768]{1,0:T(8,128)S(1)} collective-permute-done((f32[10,768]{1,0:T(8,128)S(1)}, f32[10,768]{1,0:T(8,128)S(1)}, u32[]{:S(2)}, u32[]{:S(2)}) %collective-permute-start.34) | collective-permute-done | bytes 30752 | tf_op jit(solution)/shard_map/ppermute | solution.py:106
  225.8 1.5 collective-permute-start.30
  227.3 5.8 %token_grads.3 = (bf16[392,384]{1,0:T(8,128)(2,1)S(1)}, bf16[392,384]{1,0:T(8,128)(2,1)S(1)}, bf16[392,384]{1,0:T(8,128)(2,1)S(1)}, bf16[392,384]{1,0:T(8,128)(2,1)S(1)}) custom-call(s32[8]{0:T(128)S(1)} %stack.256.index_ref, bf16[392,768]{1,0:T(8,128)(2,1)S(1)} %bitcast.82, bf16[392,768]{1,0:T(8,128)(2,1)S(1)} %collective-permute-done.20.gs, ...), custom_call_target="tpu_custom_call" | custom-call | flops 1849688064 | bytes 5922816 | tf_op jit(solution)/shard_map/token_grads/pallas_call | solution.py:190
  233.7 11.7 %weight_grad.3 = bf16[768,3072]{1,0:T(8,128)(2,1)} custom-call(s32[1]{0:T(128)} %bitcast.34.core_ref, bf16[2,4,392,384]{3,2,1,0:T(8,128)(2,1)} %pad_maximum_fusion.1.o, bf16[2,4,392,384]{3,2,1,0:T(8,128)(2,1)} %collective-permute-done.32.s, bf16[392,768]{1,0:T(8,128)(2,1)S(1)} %bitcast.86, bf16[392,768]{1,0:T(8,128)(2,1)S(1)} %collective-permute-done.33.r), custom_call_target="tpu_custom_call" | custom-call | flops 3699376128 | bytes 11943936 | tf_op jit(solution)/shard_map/weight_grad/pallas_call | solution.py:243
  245.4 1.5 collective-permute-start.24
  247.5 5.8 %token_grads.2 = (bf16[392,384]{1,0:T(8,128)(2,1)S(1)}, bf16[392,384]{1,0:T(8,128)(2,1)S(1)}, bf16[392,384]{1,0:T(8,128)(2,1)S(1)}, bf16[392,384]{1,0:T(8,128)(2,1)S(1)}) custom-call(s32[8]{0:T(128)S(1)} %stack.232.index_ref, bf16[392,768]{1,0:T(8,128)(2,1)S(1)} %bitcast.83, bf16[392,768]{1,0:T(8,128)(2,1)S(1)} %collective-permute-done.20.gs, ...), custom_call_target="tpu_custom_call" | custom-call | flops 1849688064 | bytes 5922816 | tf_op jit(solution)/shard_map/token_grads/pallas_call | solution.py:190
  253.3 1.5 collective-permute-start.21
  255.5 1.4 collective-permute-start.23
  256.9 5.0 %collective-permute-done.26 = bf16[392,384]{1,0:T(8,128)(2,1)S(1)} collective-permute-done((bf16[392,384]{1,0:T(8,128)(2,1)S(1)}, bf16[392,384]{1,0:T(8,128)(2,1)S(1)}, u32[]{:S(2)}, u32[]{:S(2)}) %collective-permute-start.26) | collective-permute-done | bytes 301088 | tf_op jit(solution)/shard_map/ppermute | solution.py:98
  262.0 3.9 %collective-permute-start.27 = (bf16[392,384]{1,0:T(8,128)(2,1)S(1)}, bf16[392,384]{1,0:T(8,128)(2,1)S(1)}, u32[]{:S(2)}, u32[]{:S(2)}) collective-permute-start(bf16[392,384]{1,0:T(8,128)(2,1)S(1)} %add_convert_fusion.2), channel_id=1, source_target_pairs={{0,12},{1,13},{2,14},{3,15},{4,0},{5,1},{6,2},{7,3},{8,4},{9,5},{1... | collective-permute-start | bytes 903176 | tf_op jit(solution)/shard_map/ppermute | solution.py:94
  265.9 10.8 %weight_grad.2 = bf16[3072,768]{1,0:T(8,128)(2,1)} custom-call(s32[1]{0:T(128)} %bitcast.34.core_ref, bf16[2,4,392,384]{3,2,1,0:T(8,128)(2,1)} %pad_maximum_fusion.o, bf16[2,4,392,384]{3,2,1,0:T(8,128)(2,1)} %collective-permute-done.29.s, bf16[392,768]{1,0:T(8,128)(2,1)S(1)} %bitcast.84, bf16[392,768]{1,0:T(8,128)(2,1)S(1)} %collective-permute-done.30.r), custom_call_target="tpu_custom_call" | custom-call | flops 3699376128 | bytes 11943936 | tf_op jit(solution)/shard_map/weight_grad/pallas_call | solution.py:243
  276.7 3.5 %collective-permute-done.27 = bf16[392,384]{1,0:T(8,128)(2,1)S(1)} collective-permute-done((bf16[392,384]{1,0:T(8,128)(2,1)S(1)}, bf16[392,384]{1,0:T(8,128)(2,1)S(1)}, u32[]{:S(2)}, u32[]{:S(2)}) %collective-permute-start.27) | collective-permute-done | bytes 301088 | tf_op jit(solution)/shard_map/ppermute | solution.py:94
  280.2 0.9 add_convert_fusion.1
  (101 shorter events, 10.0 us)
Async XLA Ops:
  5.5 125.4 %collective-permute-start.16 = (bf16[3072,768]{1,0:T(8,128)(2,1)}, bf16[3072,768]{1,0:T(8,128)(2,1)}, u32[]{:S(2)}, u32[]{:S(2)}) collective-permute-start(bf16[3072,768]{1,0:T(8,128)(2,1)} %bitcast.24), channel_id=1, source_target_pairs={{0,1},{1,0},{2,3},{3,2},{4,5},{5,4},{6,7},{7,6},{8,9},{9,8},{10,11... | collective-permute-start | bytes 14155784 | tf_op jit(solution)/shard_map/ppermute | solution.py:102
  53.0 5.8 %copy-start.1 = (bf16[392,384]{1,0:T(8,128)(2,1)S(1)}, bf16[392,384]{1,0:T(8,128)(2,1)}, u32[]{:S(2)}) copy-start(bf16[392,384]{1,0:T(8,128)(2,1)} %refs_0_.2) | copy-start | bytes 903172
  53.0 10.7 %copy-start.3 = (f32[9,768]{1,0:T(8,128)S(1)}, f32[9,768]{1,0:T(8,128)}, u32[]{:S(2)}) copy-start(f32[9,768]{1,0:T(8,128)} %param.10) | copy-start | bytes 82948
  58.7 84.4 %collective-permute-start.14 = (bf16[768,3072]{1,0:T(8,128)(2,1)}, bf16[768,3072]{1,0:T(8,128)(2,1)}, u32[]{:S(2)}, u32[]{:S(2)}) collective-permute-start(bf16[768,3072]{1,0:T(8,128)(2,1)} %bitcast.59), channel_id=1, source_target_pairs={{0,1},{1,0},{2,3},{3,2},{4,5},{5,4},{6,7},{7,6},{8,9},{9,8},{10,11... | collective-permute-start | bytes 14155784 | tf_op jit(solution)/shard_map/ppermute | solution.py:102
  58.7 12.4 %collective-permute-start = (bf16[392,384]{1,0:T(8,128)(2,1)S(1)}, bf16[392,384]{1,0:T(8,128)(2,1)S(1)}, u32[]{:S(2)}, u32[]{:S(2)}) collective-permute-start(bf16[392,384]{1,0:T(8,128)(2,1)S(1)} %copy-done.1), channel_id=1, source_target_pairs={{0,4},{1,5},{2,6},{3,7},{4,8},{5,9},{6,10},{7,11},{8,12},{9,13},{1... | collective-permute-start | bytes 903176 | tf_op jit(solution)/shard_map/ppermute | solution.py:94
  61.8 9.3 %collective-permute-start.1 = (bf16[392,384]{1,0:T(8,128)(2,1)S(1)}, bf16[392,384]{1,0:T(8,128)(2,1)S(1)}, u32[]{:S(2)}, u32[]{:S(2)}) collective-permute-start(bf16[392,384]{1,0:T(8,128)(2,1)S(1)} %copy-done.1), channel_id=1, source_target_pairs={{0,2},{1,3},{2,0},{3,1},{4,6},{5,7},{6,4},{7,5},{8,10},{9,11},{10,... | collective-permute-start | bytes 903176 | tf_op jit(solution)/shard_map/ppermute | solution.py:98
  63.8 28.0 %copy-start = (bf16[392,384]{1,0:T(8,128)(2,1)S(1)}, bf16[392,384]{1,0:T(8,128)(2,1)}, u32[]{:S(2)}) copy-start(bf16[392,384]{1,0:T(8,128)(2,1)} %refs_0_.1) | copy-start | bytes 903172
  71.1 10.3 %collective-permute-start.2 = (bf16[392,384]{1,0:T(8,128)(2,1)S(1)}, bf16[392,384]{1,0:T(8,128)(2,1)S(1)}, u32[]{:S(2)}, u32[]{:S(2)}) collective-permute-start(bf16[392,384]{1,0:T(8,128)(2,1)S(1)} %collective-permute-done.refs_1_), channel_id=1, source_target_pairs={{0,4},{1,5},{2,6},{3,7},{4,8},{5,9},{6,10},{7,11},{8,12},{9,13},{1... | collective-permute-start | bytes 903176 | tf_op jit(solution)/shard_map/ppermute | solution.py:94
  72.1 9.3 %collective-permute-start.3 = (bf16[392,384]{1,0:T(8,128)(2,1)S(1)}, bf16[392,384]{1,0:T(8,128)(2,1)S(1)}, u32[]{:S(2)}, u32[]{:S(2)}) collective-permute-start(bf16[392,384]{1,0:T(8,128)(2,1)S(1)} %collective-permute-done.refs_1_), channel_id=1, source_target_pairs={{0,2},{1,3},{2,0},{3,1},{4,6},{5,7},{6,4},{7,5},{8,10},{9,11},{10,... | collective-permute-start | bytes 903176 | tf_op jit(solution)/shard_map/ppermute | solution.py:98
  81.4 9.4 %collective-permute-start.4 = (bf16[392,384]{1,0:T(8,128)(2,1)S(1)}, bf16[392,384]{1,0:T(8,128)(2,1)S(1)}, u32[]{:S(2)}, u32[]{:S(2)}) collective-permute-start(bf16[392,384]{1,0:T(8,128)(2,1)S(1)} %collective-permute-done.2.refs_2_), channel_id=1, source_target_pairs={{0,4},{1,5},{2,6},{3,7},{4,8},{5,9},{6,10},{7,11},{8,12},{9,13},{1... | collective-permute-start | bytes 903176 | tf_op jit(solution)/shard_map/ppermute | solution.py:94
  81.4 9.4 %collective-permute-start.5 = (bf16[392,384]{1,0:T(8,128)(2,1)S(1)}, bf16[392,384]{1,0:T(8,128)(2,1)S(1)}, u32[]{:S(2)}, u32[]{:S(2)}) collective-permute-start(bf16[392,384]{1,0:T(8,128)(2,1)S(1)} %collective-permute-done.2.refs_2_), channel_id=1, source_target_pairs={{0,2},{1,3},{2,0},{3,1},{4,6},{5,7},{6,4},{7,5},{8,10},{9,11},{10,... | collective-permute-start | bytes 903176 | tf_op jit(solution)/shard_map/ppermute | solution.py:98
  90.8 6.8 %collective-permute-start.7 = (bf16[392,384]{1,0:T(8,128)(2,1)S(1)}, bf16[392,384]{1,0:T(8,128)(2,1)S(1)}, u32[]{:S(2)}, u32[]{:S(2)}) collective-permute-start(bf16[392,384]{1,0:T(8,128)(2,1)S(1)} %collective-permute-done.4.refs_3_), channel_id=1, source_target_pairs={{0,2},{1,3},{2,0},{3,1},{4,6},{5,7},{6,4},{7,5},{8,10},{9,11},{10,... | collective-permute-start | bytes 903176 | tf_op jit(solution)/shard_map/ppermute | solution.py:98
  91.8 8.6 %collective-permute-start.6 = (bf16[392,384]{1,0:T(8,128)(2,1)S(1)}, bf16[392,384]{1,0:T(8,128)(2,1)S(1)}, u32[]{:S(2)}, u32[]{:S(2)}) collective-permute-start(bf16[392,384]{1,0:T(8,128)(2,1)S(1)} %copy-done), channel_id=1, source_target_pairs={{0,4},{1,5},{2,6},{3,7},{4,8},{5,9},{6,10},{7,11},{8,12},{9,13},{1... | collective-permute-start | bytes 903176 | tf_op jit(solution)/shard_map/ppermute | solution.py:94
  100.4 8.6 %collective-permute-start.8 = (bf16[392,384]{1,0:T(8,128)(2,1)S(1)}, bf16[392,384]{1,0:T(8,128)(2,1)S(1)}, u32[]{:S(2)}, u32[]{:S(2)}) collective-permute-start(bf16[392,384]{1,0:T(8,128)(2,1)S(1)} %collective-permute-done.6.refs_1_), channel_id=1, source_target_pairs={{0,4},{1,5},{2,6},{3,7},{4,8},{5,9},{6,10},{7,11},{8,12},{9,13},{1... | collective-permute-start | bytes 903176 | tf_op jit(solution)/shard_map/ppermute | solution.py:94
  100.4 11.6 %collective-permute-start.11 = (bf16[392,384]{1,0:T(8,128)(2,1)S(1)}, bf16[392,384]{1,0:T(8,128)(2,1)S(1)}, u32[]{:S(2)}, u32[]{:S(2)}) collective-permute-start(bf16[392,384]{1,0:T(8,128)(2,1)S(1)} %collective-permute-done.6.refs_1_), channel_id=1, source_target_pairs={{0,2},{1,3},{2,0},{3,1},{4,6},{5,7},{6,4},{7,5},{8,10},{9,11},{10,... | collective-permute-start | bytes 903176 | tf_op jit(solution)/shard_map/ppermute | solution.py:98
  101.4 10.4 %collective-permute-start.9 = (bf16[392,384]{1,0:T(8,128)(2,1)S(1)}, bf16[392,384]{1,0:T(8,128)(2,1)S(1)}, u32[]{:S(2)}, u32[]{:S(2)}) collective-permute-start(bf16[392,384]{1,0:T(8,128)(2,1)S(1)} %copy-done), channel_id=1, source_target_pairs={{0,2},{1,3},{2,0},{3,1},{4,6},{5,7},{6,4},{7,5},{8,10},{9,11},{10,... | collective-permute-start | bytes 903176 | tf_op jit(solution)/shard_map/ppermute | solution.py:98
  111.8 10.2 %collective-permute-start.10 = (bf16[392,384]{1,0:T(8,128)(2,1)S(1)}, bf16[392,384]{1,0:T(8,128)(2,1)S(1)}, u32[]{:S(2)}, u32[]{:S(2)}) collective-permute-start(bf16[392,384]{1,0:T(8,128)(2,1)S(1)} %collective-permute-done.8.refs_0_), channel_id=1, source_target_pairs={{0,4},{1,5},{2,6},{3,7},{4,8},{5,9},{6,10},{7,11},{8,12},{9,13},{1... | collective-permute-start | bytes 903176 | tf_op jit(solution)/shard_map/ppermute | solution.py:94
  122.1 8.6 %collective-permute-start.12 = (bf16[392,384]{1,0:T(8,128)(2,1)S(1)}, bf16[392,384]{1,0:T(8,128)(2,1)S(1)}, u32[]{:S(2)}, u32[]{:S(2)}) collective-permute-start(bf16[392,384]{1,0:T(8,128)(2,1)S(1)} %collective-permute-done.11.refs_3_), channel_id=1, source_target_pairs={{0,4},{1,5},{2,6},{3,7},{4,8},{5,9},{6,10},{7,11},{8,12},{9,13},{1... | collective-permute-start | bytes 903176 | tf_op jit(solution)/shard_map/ppermute | solution.py:94
  122.1 8.7 %collective-permute-start.13 = (bf16[392,384]{1,0:T(8,128)(2,1)S(1)}, bf16[392,384]{1,0:T(8,128)(2,1)S(1)}, u32[]{:S(2)}, u32[]{:S(2)}) collective-permute-start(bf16[392,384]{1,0:T(8,128)(2,1)S(1)} %collective-permute-done.10.refs_1_), channel_id=1, source_target_pairs={{0,2},{1,3},{2,0},{3,1},{4,6},{5,7},{6,4},{7,5},{8,10},{9,11},{10,... | collective-permute-start | bytes 903176 | tf_op jit(solution)/shard_map/ppermute | solution.py:98
  140.9 15.6 %collective-permute-start.17 = (f32[392,768]{1,0:T(8,128)S(1)}, f32[392,768]{1,0:T(8,128)S(1)}, u32[]{:S(2)}, u32[]{:S(2)}) collective-permute-start(f32[392,768]{1,0:T(8,128)S(1)} %get-tuple-element.50), channel_id=1, source_target_pairs={{0,1},{1,0},{2,3},{3,2},{4,5},{5,4},{6,7},{7,6},{8,9},{9,8},{10,11... | collective-permute-start | bytes 3612680 | tf_op jit(solution)/shard_map/ppermute | solution.py:102
  141.4 29.4 %collective-permute-start.31 = (bf16[4,392,384]{2,1,0:T(8,128)(2,1)S(1)}, bf16[4,392,384]{2,1,0:T(8,128)(2,1)S(1)}, u32[]{:S(2)}, u32[]{:S(2)}) collective-permute-start(bf16[4,392,384]{2,1,0:T(8,128)(2,1)S(1)} %pad_maximum_fusion.3), channel_id=1, source_target_pairs={{0,16},{16,0},{1,17},{17,1},{2,18},{18,2},{3,19},{19,3},{4,20},{20... | collective-permute-start | bytes 3612680 | tf_op jit(solution)/shard_map/ppermute | solution.py:106
  154.8 17.7 %collective-permute-start.15 = (f32[392,768]{1,0:T(8,128)S(1)}, f32[392,768]{1,0:T(8,128)S(1)}, u32[]{:S(2)}, u32[]{:S(2)}) collective-permute-start(f32[392,768]{1,0:T(8,128)S(1)} %get-tuple-element.45), channel_id=1, source_target_pairs={{0,1},{1,0},{2,3},{3,2},{4,5},{5,4},{6,7},{7,6},{8,9},{9,8},{10,11... | collective-permute-start | bytes 3612680 | tf_op jit(solution)/shard_map/ppermute | solution.py:102
  155.5 47.9 %collective-permute-start.28 = (bf16[4,392,384]{2,1,0:T(8,128)(2,1)S(1)}, bf16[4,392,384]{2,1,0:T(8,128)(2,1)S(1)}, u32[]{:S(2)}, u32[]{:S(2)}) collective-permute-start(bf16[4,392,384]{2,1,0:T(8,128)(2,1)S(1)} %pad_maximum_fusion.2), channel_id=1, source_target_pairs={{0,16},{16,0},{1,17},{17,1},{2,18},{18,2},{3,19},{19,3},{4,20},{20... | collective-permute-start | bytes 3612680 | tf_op jit(solution)/shard_map/ppermute | solution.py:106
  156.7 41.3 %collective-permute-start.18 = (bf16[1,56,768]{2,1,0:T(8,128)(2,1)S(1)}, bf16[1,56,768]{2,1,0:T(8,128)(2,1)S(1)}, u32[]{:S(2)}, u32[]{:S(2)}) collective-permute-start(bf16[1,56,768]{2,1,0:T(8,128)(2,1)S(1)} %fusion.33), channel_id=1, source_target_pairs={{0,16},{16,0},{1,17},{17,1},{2,18},{18,2},{3,19},{19,3},{4,20},{20... | collective-permute-start | bytes 258056 | tf_op jit(solution)/shard_map/ppermute | solution.py:106
  172.5 61.2 %collective-permute-start.32 = (bf16[2,4,392,384]{3,2,1,0:T(8,128)(2,1)}, bf16[2,4,392,384]{3,2,1,0:T(8,128)(2,1)}, u32[]{:S(2)}, u32[]{:S(2)}) collective-permute-start(bf16[2,4,392,384]{3,2,1,0:T(8,128)(2,1)} %pad_maximum_fusion.1.o), channel_id=1, source_target_pairs={{0,1},{1,0},{2,3},{3,2},{4,5},{5,4},{6,7},{7,6},{8,9},{9,8},{10,11... | collective-permute-start | bytes 7225352 | tf_op jit(solution)/shard_map/ppermute | solution.py:102
  198.1 0.7 copy-start.4
  201.9 4.6 %collective-permute-start.19 = (bf16[1,56,768]{2,1,0:T(8,128)(2,1)S(1)}, bf16[1,56,768]{2,1,0:T(8,128)(2,1)S(1)}, u32[]{:S(2)}, u32[]{:S(2)}) collective-permute-start(bf16[1,56,768]{2,1,0:T(8,128)(2,1)S(1)} %slice_select_fusion), channel_id=1, source_target_pairs={{0,16},{16,0},{1,17},{17,1},{2,18},{18,2},{3,19},{19,3},{4,20},{20... | collective-permute-start | bytes 258056 | tf_op jit(solution)/shard_map/ppermute | solution.py:106
  205.2 56.9 %collective-permute-start.29 = (bf16[2,4,392,384]{3,2,1,0:T(8,128)(2,1)}, bf16[2,4,392,384]{3,2,1,0:T(8,128)(2,1)}, u32[]{:S(2)}, u32[]{:S(2)}) collective-permute-start(bf16[2,4,392,384]{3,2,1,0:T(8,128)(2,1)} %pad_maximum_fusion.o), channel_id=1, source_target_pairs={{0,1},{1,0},{2,3},{3,2},{4,5},{5,4},{6,7},{7,6},{8,9},{9,8},{10,11... | collective-permute-start | bytes 7225352 | tf_op jit(solution)/shard_map/ppermute | solution.py:102
  207.6 19.7 %collective-permute-start.20 = (bf16[392,768]{1,0:T(8,128)(2,1)S(1)}, bf16[392,768]{1,0:T(8,128)(2,1)S(1)}, u32[]{:S(2)}, u32[]{:S(2)}) collective-permute-start(bf16[392,768]{1,0:T(8,128)(2,1)S(1)} %bitcast.80), channel_id=1, source_target_pairs={{0,1},{1,0},{2,3},{3,2},{4,5},{5,4},{6,7},{7,6},{8,9},{9,8},{10,11... | collective-permute-start | bytes 1806344 | tf_op jit(solution)/shard_map/ppermute | solution.py:102
  208.0 25.7 %collective-permute-start.33 = (bf16[392,768]{1,0:T(8,128)(2,1)S(1)}, bf16[392,768]{1,0:T(8,128)(2,1)S(1)}, u32[]{:S(2)}, u32[]{:S(2)}) collective-permute-start(bf16[392,768]{1,0:T(8,128)(2,1)S(1)} %bitcast.85), channel_id=1, source_target_pairs={{0,16},{16,0},{1,17},{17,1},{2,18},{18,2},{3,19},{19,3},{4,20},{20... | collective-permute-start | bytes 1806344 | tf_op jit(solution)/shard_map/ppermute | solution.py:106
  209.8 15.3 %collective-permute-start.34 = (f32[10,768]{1,0:T(8,128)S(1)}, f32[10,768]{1,0:T(8,128)S(1)}, u32[]{:S(2)}, u32[]{:S(2)}) collective-permute-start(f32[10,768]{1,0:T(8,128)S(1)} %stack.291), channel_id=1, source_target_pairs={{0,16},{16,0},{1,17},{17,1},{2,18},{18,2},{3,19},{19,3},{4,20},{20... | collective-permute-start | bytes 92168 | tf_op jit(solution)/shard_map/ppermute | solution.py:106
  225.2 7.9 %copy-start.2 = (f32[10,768]{1,0:T(8,128)}, f32[10,768]{1,0:T(8,128)S(1)}, u32[]{:S(2)}) copy-start(f32[10,768]{1,0:T(8,128)S(1)} %add.464) | copy-start | bytes 92164
  225.8 40.2 %collective-permute-start.30 = (bf16[392,768]{1,0:T(8,128)(2,1)S(1)}, bf16[392,768]{1,0:T(8,128)(2,1)S(1)}, u32[]{:S(2)}, u32[]{:S(2)}) collective-permute-start(bf16[392,768]{1,0:T(8,128)(2,1)S(1)} %bitcast.81), channel_id=1, source_target_pairs={{0,16},{16,0},{1,17},{17,1},{2,18},{18,2},{3,19},{19,3},{4,20},{20... | collective-permute-start | bytes 1806344 | tf_op jit(solution)/shard_map/ppermute | solution.py:106
  233.1 20.2 %collective-permute-start.22 = (bf16[392,384]{1,0:T(8,128)(2,1)S(1)}, bf16[392,384]{1,0:T(8,128)(2,1)S(1)}, u32[]{:S(2)}, u32[]{:S(2)}) collective-permute-start(bf16[392,384]{1,0:T(8,128)(2,1)S(1)} %get-tuple-element.54), channel_id=1, source_target_pairs={{0,2},{1,3},{2,0},{3,1},{4,6},{5,7},{6,4},{7,5},{8,10},{9,11},{10,... | collective-permute-start | bytes 903176 | tf_op jit(solution)/shard_map/ppermute | solution.py:98
  245.4 10.1 %collective-permute-start.24 = (bf16[392,384]{1,0:T(8,128)(2,1)S(1)}, bf16[392,384]{1,0:T(8,128)(2,1)S(1)}, u32[]{:S(2)}, u32[]{:S(2)}) collective-permute-start(bf16[392,384]{1,0:T(8,128)(2,1)S(1)} %get-tuple-element.56), channel_id=1, source_target_pairs={{0,2},{1,3},{2,0},{3,1},{4,6},{5,7},{6,4},{7,5},{8,10},{9,11},{10,... | collective-permute-start | bytes 903176 | tf_op jit(solution)/shard_map/ppermute | solution.py:98
  246.9 15.0 %collective-permute-start.26 = (bf16[392,384]{1,0:T(8,128)(2,1)S(1)}, bf16[392,384]{1,0:T(8,128)(2,1)S(1)}, u32[]{:S(2)}, u32[]{:S(2)}) collective-permute-start(bf16[392,384]{1,0:T(8,128)(2,1)S(1)} %get-tuple-element.58), channel_id=1, source_target_pairs={{0,2},{1,3},{2,0},{3,1},{4,6},{5,7},{6,4},{7,5},{8,10},{9,11},{10,... | collective-permute-start | bytes 903176 | tf_op jit(solution)/shard_map/ppermute | solution.py:98
  253.3 23.4 %collective-permute-start.21 = (bf16[392,384]{1,0:T(8,128)(2,1)S(1)}, bf16[392,384]{1,0:T(8,128)(2,1)S(1)}, u32[]{:S(2)}, u32[]{:S(2)}) collective-permute-start(bf16[392,384]{1,0:T(8,128)(2,1)S(1)} %get-tuple-element.52), channel_id=1, source_target_pairs={{0,2},{1,3},{2,0},{3,1},{4,6},{5,7},{6,4},{7,5},{8,10},{9,11},{10,... | collective-permute-start | bytes 903176 | tf_op jit(solution)/shard_map/ppermute | solution.py:98
  255.5 21.2 %collective-permute-start.23 = (bf16[392,384]{1,0:T(8,128)(2,1)S(1)}, bf16[392,384]{1,0:T(8,128)(2,1)S(1)}, u32[]{:S(2)}, u32[]{:S(2)}) collective-permute-start(bf16[392,384]{1,0:T(8,128)(2,1)S(1)} %add_convert_fusion.4), channel_id=1, source_target_pairs={{0,8},{1,9},{2,10},{3,11},{4,12},{5,13},{6,14},{7,15},{8,0},{9,1},... | collective-permute-start | bytes 903176 | tf_op jit(solution)/shard_map/ppermute | solution.py:94
  262.0 14.8 %collective-permute-start.25 = (bf16[392,384]{1,0:T(8,128)(2,1)S(1)}, bf16[392,384]{1,0:T(8,128)(2,1)S(1)}, u32[]{:S(2)}, u32[]{:S(2)}) collective-permute-start(bf16[392,384]{1,0:T(8,128)(2,1)S(1)} %add_convert_fusion.3), channel_id=1, source_target_pairs={{0,4},{1,5},{2,6},{3,7},{4,8},{5,9},{6,10},{7,11},{8,12},{9,13},{1... | collective-permute-start | bytes 903176 | tf_op jit(solution)/shard_map/ppermute | solution.py:94
  262.0 18.2 %collective-permute-start.27 = (bf16[392,384]{1,0:T(8,128)(2,1)S(1)}, bf16[392,384]{1,0:T(8,128)(2,1)S(1)}, u32[]{:S(2)}, u32[]{:S(2)}) collective-permute-start(bf16[392,384]{1,0:T(8,128)(2,1)S(1)} %add_convert_fusion.2), channel_id=1, source_target_pairs={{0,12},{1,13},{2,14},{3,15},{4,0},{5,1},{6,2},{7,3},{8,4},{9,5},{1... | collective-permute-start | bytes 903176 | tf_op jit(solution)/shard_map/ppermute | solution.py:94

commit v2 on v1

v2 whole, which is shorter than its diff:
```python
import jax
import jax.numpy as jnp
from jax import lax
from jax.experimental import pallas as pl
from jax.experimental.pallas import tpu as pltpu
from jax.sharding import PartitionSpec as P

GW = 56
NZ, NX, NC = 4, 2, 2

OFFSETS = [(-1, -1), (-1, 0), (-1, 1), (0, -1), (0, 0), (0, 1), (1, -1), (1, 0), (1, 1)]

BF = jnp.bfloat16
F32 = jnp.float32


def gelu_parts(pre):
    inner = 0.7978845608 * (pre + 0.044715 * pre * pre * pre)
    tanh_val = jnp.tanh(inner)
    value = 0.5 * pre * (1.0 + tanh_val)
    slope = 0.5 * (1.0 + tanh_val) + 0.5 * pre * (1.0 - tanh_val * tanh_val) * 0.7978845608 * (
        1.0 + 3.0 * 0.044715 * pre * pre
    )
    return (value, slope)


def padded_2(block, sides, width):
    for axis, dim in sides:
        count = lax.axis_size(axis)
        forward = [(i, i + 1) for i in range(count - 1)]
        backward = [(target, source) for source, target in forward]
        low = lax.ppermute(
            lax.slice_in_dim(block, block.shape[dim] - width, None, axis=dim), axis, forward
        )
        high = lax.ppermute(lax.slice_in_dim(block, 0, width, axis=dim), axis, backward)
        block = jnp.concatenate([low, block, high], axis=dim)
    return block


def shards_any(tokens, grad_out, w_in, w_out, conv_kernel, conv_bias):
    tok_rows = tokens.shape[0]
    grid_rows = tok_rows // GW
    ff_local = w_in.shape[1]
    full_tokens, full_grad = (
        lax.all_gather(tokens, "tensor", axis=1, tiled=True),
        lax.all_gather(grad_out, "tensor", axis=1, tiled=True),
    )
    hidden_acc = jnp.dot(full_tokens, w_in, preferred_element_type=F32)
    grad_act = lax.dot_general(full_grad, w_out, (((1,), (1,)), ((), ())), preferred_element_type=F32)
    hidden = hidden_acc.astype(BF).reshape(grid_rows, GW, ff_local)
    rimmed = padded_2(hidden, (("space", 0),), 1)
    padded = jnp.pad(rimmed, ((0, 0), (1, 1), (0, 0))).astype(F32)
    pre = jnp.zeros((grid_rows, GW, ff_local), F32) + conv_bias
    for index, (da, db) in enumerate(OFFSETS):
        pre = pre + conv_kernel[index] * padded[1 + da : 1 + da + grid_rows, 1 + db : 1 + db + GW]
    act, slope = gelu_parts(pre)
    act = act.astype(BF).reshape(tok_rows, ff_local)
    grad_pre = (grad_act.reshape(grid_rows, GW, ff_local) * slope).astype(BF)
    out_term = lax.dot_general(act, full_grad, (((0,), (0,)), ((), ())), preferred_element_type=F32)
    grad_f = grad_pre.astype(F32)
    kernel_rows = []
    for index, (da, db) in enumerate(OFFSETS):
        kernel_rows.append(
            jnp.sum(grad_f * padded[1 + da : 1 + da + grid_rows, 1 + db : 1 + db + GW], axis=(0, 1))
        )
    kernel_terms = jnp.stack(kernel_rows)
    bias_term = jnp.sum(grad_f, axis=(0, 1))
    grad_kernel, grad_bias = lax.psum((kernel_terms, bias_term), "space")
    grad_rimmed = padded_2(grad_pre, (("space", 0),), 1)
    grad_padded = jnp.pad(grad_rimmed, ((0, 0), (1, 1), (0, 0))).astype(F32)
    grad_hidden = jnp.zeros((grid_rows, GW, ff_local), F32)
    for index, (da, db) in enumerate(OFFSETS):
        grad_hidden = (
            grad_hidden
            + conv_kernel[index] * grad_padded[1 - da : 1 - da + grid_rows, 1 - db : 1 - db + GW]
        )
    grad_hidden = grad_hidden.astype(BF).reshape(tok_rows, ff_local)
    in_term = lax.dot_general(full_tokens, grad_hidden, (((0,), (0,)), ((), ())), preferred_element_type=F32)
    grad_w_in = lax.psum_scatter(in_term.astype(BF), "space", scatter_dimension=0, tiled=True)
    grad_w_out = lax.psum_scatter(out_term.astype(BF), "space", scatter_dimension=1, tiled=True)
    token_terms = lax.dot_general(grad_hidden, w_in, (((1,), (1,)), ((), ())), preferred_element_type=F32)
    grad_tokens = lax.psum_scatter(token_terms.astype(BF), "tensor", scatter_dimension=1, tiled=True)
    return (grad_tokens, grad_w_in, grad_w_out, grad_kernel, grad_bias)


def dev(z, x, c):
    return (z * NX + x) * NC + c


ALL = [(z, x, c) for z in range(NZ) for x in range(NX) for c in range(NC)]


def go_z(v, k=1):
    return lax.ppermute(v, "tensor", [(dev(z, x, c), dev((z + k) % NZ, x, c)) for z, x, c in ALL])


def go_x(v):
    return lax.ppermute(v, "tensor", [(dev(z, x, c), dev(z, 1 - x, c)) for z, x, c in ALL])


def go_c(v):
    return lax.ppermute(v, "tensor", [(dev(z, x, c), dev(z, x, 1 - c)) for z, x, c in ALL])


def go_y(v):
    return lax.ppermute(v, "space", [(0, 1), (1, 0)])


PARAMS = dict(vmem_limit_bytes=48 * 1024 * 1024)
NN = (((1,), (0,)), ((), ()))
NT = (((1,), (1,)), ((), ()))
TN = (((0,), (0,)), ((), ()))


def project(core, pairs, where, w, dims, acc=None, times=None, dtype=F32):
    n = len(pairs)
    rows, bw = pairs[0][0].shape
    wide = dims is NN
    ff = w.shape[1] if wide else w.shape[0]
    index = jnp.stack([core] + list(where)).astype(jnp.int32)
    extra = [v for v in (acc, times) if v is not None]

    def body(index_ref, *refs):
        out, total = refs[-2:]
        w_ref = refs[2 * n]
        i = pl.program_id(0)
        even = index_ref[0] == 0
        for k in range(n):

            @pl.when(i == k)
            def _(k=k):
                p, q = refs[2 * k][...], refs[2 * k + 1][...]
                b = jnp.concatenate([jnp.where(even, p, q), jnp.where(even, q, p)], axis=1)
                t = lax.dot_general(b, w_ref[...], dims, preferred_element_type=F32)
                if k > 0:
                    t = t + total[...]
                elif acc is not None:
                    t = t + refs[2 * n + 1][...]
                if k < n - 1:
                    total[...] = t
                else:
                    if times is not None:
                        t = t * refs[2 * n + len(extra)][...]
                    out[...] = t.astype(dtype)

    whole = lambda i, r: (0, 0)
    if wide:
        w_spec = pl.BlockSpec((NC * bw, ff), lambda i, r: (r[1 + i], 0))
    else:
        w_spec = pl.BlockSpec((ff, NC * bw), lambda i, r: (0, r[1 + i]))
    return pl.pallas_call(
        body,
        grid_spec=pltpu.PrefetchScalarGridSpec(
            num_scalar_prefetch=1,
            grid=(n,),
            in_specs=[pl.BlockSpec((rows, bw), whole)] * (2 * n)
            + [w_spec]
            + [pl.BlockSpec((rows, ff), whole)] * len(extra),
            out_specs=pl.BlockSpec((rows, ff), whole),
            scratch_shapes=[pltpu.VMEM((rows, ff), F32)],
        ),
        out_shape=jax.ShapeDtypeStruct((rows, ff), dtype),
        compiler_params=pltpu.CompilerParams(**PARAMS),
        cost_estimate=pl.CostEstimate(
            flops=4 * n * rows * bw * ff, transcendentals=0, bytes_accessed=4 * n * bw * ff + 8 * rows * ff
        ),
        name="project",
    )(index, *[v for pair in pairs for v in pair], w, *extra)


def token_grads(gh_own, gh_sib, w_own, w_sib, where_own, where_sib, bw):
    n = len(where_own)
    rows, ff = gh_own.shape
    index = jnp.stack(list(where_own) + list(where_sib)).astype(jnp.int32)

    def body(index_ref, go, gs, wo, ws, out):
        t = lax.dot_general(go[...], wo[...], NT, preferred_element_type=F32)
        t = t + lax.dot_general(gs[...], ws[...], NT, preferred_element_type=F32)
        out[0] = t.astype(BF)

    whole = lambda i, r: (0, 0)
    return pl.pallas_call(
        body,
        grid_spec=pltpu.PrefetchScalarGridSpec(
            num_scalar_prefetch=1,
            grid=(n,),
            in_specs=[
                pl.BlockSpec((rows, ff), whole),
                pl.BlockSpec((rows, ff), whole),
                pl.BlockSpec((bw, ff), lambda i, r: (r[i], 0)),
                pl.BlockSpec((bw, ff), lambda i, r: (r[n + i], 0)),
            ],
            out_specs=pl.BlockSpec((1, rows, bw), lambda i, r: (i, 0, 0)),
        ),
        out_shape=jax.ShapeDtypeStruct((n, rows, bw), BF),
        compiler_params=pltpu.CompilerParams(**PARAMS),
        cost_estimate=pl.CostEstimate(
            flops=4 * n * rows * bw * ff, transcendentals=0, bytes_accessed=4 * n * bw * ff + 2 * n * rows * bw
        ),
        name="token_grads",
    )(index, gh_own, gh_sib, w_own, w_sib)


def pack(w, core, by_rows, bw):
    rows, cols = w.shape
    n = (rows if by_rows else cols) // (NC * bw)

    def body(core_ref, w_ref, out_ref):
        out_ref[...] = w_ref[...]

    if by_rows:
        shape, block = (n * bw, cols), (bw, cols)
        at, to = (lambda i, r: (NC * i + 1 - r[0], 0)), (lambda i, r: (i, 0))
    else:
        shape, block = (rows, n * bw), (rows, bw)
        at, to = (lambda i, r: (0, NC * i + 1 - r[0])), (lambda i, r: (0, i))
    return pl.pallas_call(
        body,
        grid_spec=pltpu.PrefetchScalarGridSpec(
            num_scalar_prefetch=1, grid=(n,), in_specs=[pl.BlockSpec(block, at)], out_specs=pl.BlockSpec(block, to)
        ),
        out_shape=jax.ShapeDtypeStruct(shape, w.dtype),
        compiler_params=pltpu.CompilerParams(**PARAMS),
        cost_estimate=pl.CostEstimate(flops=0, transcendentals=0, bytes_accessed=2 * rows * cols),
        name="pack",
    )(core.reshape(1).astype(jnp.int32), w)


def weight_grad(core, sets, left, right, by_rows, blocks, into=None):
    n = len(sets)
    rows, bw = sets[0][3][0].shape
    ff = left.shape[1]
    wide = NC * bw
    index = jnp.stack([core] + [v for q in sets for v in q[:2]]).astype(jnp.int32)
    arrays, plan = [], []
    for _, _, mine, other in sets:
        row = []
        for key, pair in mine.items():
            row.append((key, len(arrays)))
            arrays += list(pair)
        plan.append((row, len(arrays)))
        arrays += list(other)
    m = len(arrays)

    def body(index_ref, l, r, *refs):
        src = refs[:m]
        out, buf, obuf, in_sem, out_sem = refs[-5:]
        c = index_ref[0]
        spots = [pl.multiple_of(c * bw, bw), pl.multiple_of((1 - c) * bw, bw)]

        def copy(q, at, band, cc):
            return pltpu.make_async_copy(
                src[at + cc], buf.at[q % 2, band, :, pl.ds(spots[cc], bw)], in_sem.at[q % 2, band, cc]
            )

        def load(q):
            row, other = plan[q]
            for key, at in row:

                @pl.when(index_ref[2 + 2 * q] == key)
                def _(at=at):
                    for cc in range(NC):
                        copy(q, at, 0, cc).start()

            for cc in range(NC):
                copy(q, other, 1, cc).start()

        def loaded(q):
            for band in range(2):
                for cc in range(NC):
                    copy(q, plan[q][1], band, cc).wait()

        def store(q):
            place = pl.multiple_of(index_ref[1 + 2 * q] * wide, wide)
            target = out.at[pl.ds(place, wide), :] if by_rows else out.at[:, pl.ds(place, wide)]
            return pltpu.make_async_copy(obuf.at[q % 2], target, out_sem.at[q % 2])

        load(0)
        for q in range(n):
            if q + 1 < n:
                load(q + 1)
            loaded(q)
            mine, other = buf[q % 2, 0], buf[q % 2, 1]
            if by_rows:
                t = lax.dot_general(mine, l[...], TN, preferred_element_type=F32)
                t = t + lax.dot_general(other, r[...], TN, preferred_element_type=F32)
            else:
                t = lax.dot_general(l[...], mine, TN, preferred_element_type=F32)
                t = t + lax.dot_general(r[...], other, TN, preferred_element_type=F32)
            if q >= 2:
                store(q - 2).wait()
            obuf[q % 2] = t.astype(BF)
            store(q).start()
        for q in range(max(0, n - 2), n):
            store(q).wait()

    more = [] if into is None else [into]
    shape = (blocks * wide, ff) if by_rows else (ff, blocks * wide)
    anywhere = pl.BlockSpec(memory_space=pltpu.HBM)
    inside = pl.BlockSpec((rows, ff), lambda i, r: (0, 0))
    return pl.pallas_call(
        body,
        grid_spec=pltpu.PrefetchScalarGridSpec(
            num_scalar_prefetch=1,
            grid=(1,),
            in_specs=[inside, inside] + [anywhere] * (m + len(more)),
            out_specs=anywhere,
            scratch_shapes=[
                pltpu.VMEM((2, 2, rows, wide), BF),
                pltpu.VMEM((2, wide, ff) if by_rows else (2, ff, wide), BF),
                pltpu.SemaphoreType.DMA((2, 2, NC)),
                pltpu.SemaphoreType.DMA((2,)),
            ],
        ),
        out_shape=jax.ShapeDtypeStruct(shape, BF),
        input_output_aliases={3 + m: 0} if more else {},
        compiler_params=pltpu.CompilerParams(**PARAMS),
        cost_estimate=pl.CostEstimate(
            flops=4 * n * rows * wide * ff, transcendentals=0, bytes_accessed=4 * n * rows * wide + 2 * n * wide * ff
        ),
        name="weight_grad",
    )(index, left, right, *arrays, *more)


def rims(block, recv, first_band):
    zero = jnp.zeros_like(recv)
    low = jnp.where(first_band, zero, recv)
    high = jnp.where(first_band, recv, zero)
    return jnp.concatenate([low, block, high], axis=0)


def pick(j, choices):
    items = list(choices.items())
    value = items[-1][1]
    for key, array in items[:-1]:
        value = jnp.where(j == key, array, value)
    return value


def shards(tokens, grad_out, w_in, w_out, conv_kernel, conv_bias):
    rows, bw = tokens.shape
    grid_rows = rows // GW
    ff = w_in.shape[1]
    s = lax.axis_index("space")
    t = lax.axis_index("tensor")
    z, x, c = t // (NX * NC), (t // NC) % NX, t % NC
    first = s == 0
    bar = lax.optimization_barrier

    def sib_at(zz, xx):
        return zz * NX + xx

    def own_at(zz, xx):
        return (zz * NX + xx) * NC + c

    def part(w, pieces, dims, **more):
        where = [sib_at((z - j) % NZ, x if same == 0 else 1 - x) for _, _, j, same in pieces]
        return project(c, [p[:2] for p in pieces], where, w, dims, **more)

    half, low = z // (NZ // 2), z % (NZ // 2)

    def places(side):
        l1 = jnp.where(half == side, low, 1)
        z1, z2 = side * (NZ // 2) + l1, side * (NZ // 2) + 1 - l1
        return l1, (z - z1) % NZ, (z - z2) % NZ

    _, j1, j2 = places(1 - s)
    l1, k1, k2 = places(s)
    l2 = 1 - l1
    blocks = NZ // 2 * NX

    a0 = tokens
    a1, e0, a0s = go_z(a0), go_x(a0), go_c(a0)
    pack_in = pack(w_in, c, True, bw)
    a1, e0, a0s, pack_in = bar((a1, e0, a0s, pack_in))

    a2, e1, a1s, e0s, w_in_sib = go_z(a1), go_x(a1), go_c(a1), go_c(e0), go_c(pack_in)
    a2, e1, a1s, e0s, w_in_sib = bar((a2, e1, a1s, e0s, w_in_sib))

    a3, e2, a2s, e1s = go_z(a2), go_x(a2), go_c(a2), go_c(e1)
    ya1 = go_y(pick(j1, {0: a0, 1: a1, 2: a2}))
    acc = part(w_in, [(a0, a0s, 0, 0), (e0, e0s, 0, 1), (a1, a1s, 1, 0)], NN)
    a3, e2, a2s, e1s, ya1, acc, b0 = bar((a3, e2, a2s, e1s, ya1, acc, grad_out))

    b1, e3, a3s, e2s = go_z(b0), go_x(a3), go_c(a3), go_c(e2)
    ye1 = go_y(pick(j1, {0: e0, 1: e1, 2: e2}))
    b1, e3, a3s, e2s, ye1, acc, b0 = bar((b1, e3, a3s, e2s, ye1, acc, b0))

    e3s = go_c(e3)
    b2, f0, b0s = go_z(b1), go_x(b0), go_c(b0)
    ya2 = go_y(pick(j2, {1: a1, 2: a2, 3: a3}))
    hidden = part(
        w_in,
        [(a2, a2s, 2, 0), (e1, e1s, 1, 1), (a3, a3s, 3, 0), (e2, e2s, 2, 1), (e3, e3s, 3, 1)],
        NN, acc=acc, dtype=BF,
    )
    b2, f0, b0s, ya2, e3s, hidden = bar((b2, f0, b0s, ya2, e3s, hidden))

    hidden = hidden.reshape(grid_rows, GW, ff)
    b3, f1, b1s, f0s = go_z(b2), go_x(b1), go_c(b1), go_c(f0)
    edge = jnp.where(first, hidden[grid_rows - 1 :], hidden[:1]).reshape(GW * ff // bw, bw)
    sent = jnp.concatenate([pick(j2, {1: e1, 2: e2, 3: e3}), edge], axis=0)
    came = go_y(sent)
    b3, f1, b1s, f0s, came = bar((b3, f1, b1s, f0s, came))

    ye2, halo = came[:rows], came[rows:].reshape(1, GW, ff)
    f2, f3, b2s, b3s = go_z(f1), go_x(b3), go_c(b2), go_c(b3)
    yb1 = go_y(pick(j1, {0: b0, 1: b1, 2: b2}))
    acc = part(w_out, [(b0, b0s, 0, 0), (b1, b1s, 1, 0), (f0, f0s, 0, 1), (b2, b2s, 2, 0)], NT)
    f2, f3, b2s, b3s, yb1, acc, ye2, halo = bar((f2, f3, b2s, b3s, yb1, acc, ye2, halo))

    f1s, f2s, f3s, ya1s = go_c(f1), go_c(f2), go_c(f3), go_c(ya1)
    yb2 = go_y(pick(j2, {1: b1, 2: b2, 3: b3}))
    rimmed = rims(hidden, halo, first)
    padded = jnp.pad(rimmed, ((0, 0), (1, 1), (0, 0))).astype(F32)
    pre = jnp.zeros((grid_rows, GW, ff), F32) + conv_bias
    for index, (da, db) in enumerate(OFFSETS):
        pre = pre + conv_kernel[index] * padded[1 + da : 1 + da + grid_rows, 1 + db : 1 + db + GW]
    act, slope = gelu_parts(pre)
    act, slope = act.astype(BF).reshape(rows, ff), slope.reshape(rows, ff)
    grad_pre = part(
        w_out,
        [(b3, b3s, 3, 0), (f1, f1s, 1, 1), (f2, f2s, 2, 1), (f3, f3s, 3, 1)],
        NT, acc=acc, times=slope, dtype=BF,
    )
    grad_pre, yb2, f1s, f2s, f3s, ya1s, act = bar((grad_pre, yb2, f1s, f2s, f3s, ya1s, act))

    grad_pre = grad_pre.reshape(grid_rows, GW, ff)
    halo = go_y(jnp.where(first, grad_pre[grid_rows - 1 :], grad_pre[:1]))
    yf1 = go_y(pick(j1, {0: f0, 1: f1, 2: f2}))
    ya2s, ye1s = go_c(ya2), go_c(ye1)
    halo, ya2s, ye1s, act = bar((halo, ya2s, ye1s, act))

    grad_rimmed = rims(grad_pre, halo, first)
    grad_padded = jnp.pad(grad_rimmed, ((0, 0), (1, 1), (0, 0))).astype(F32)
    grad_hidden = jnp.zeros((grid_rows, GW, ff), F32)
    for index, (da, db) in enumerate(OFFSETS):
        grad_hidden = (
            grad_hidden
            + conv_kernel[index] * grad_padded[1 - da : 1 - da + grid_rows, 1 - db : 1 - db + GW]
        )
    grad_hidden = grad_hidden.astype(BF).reshape(rows, ff)
    gh_sib, ye2s = go_c(grad_hidden), go_c(ye2)
    yf2 = go_y(pick(j2, {1: f1, 2: f2, 3: f3}))
    order = [2, 1, 3, 0]
    zd = [(z + j) % NZ for j in order]

    def grads(which, xx):
        return token_grads(
            grad_hidden, gh_sib, w_in, w_in_sib,
            [own_at(zd[k], xx) for k in which], [sib_at(zd[k], xx) for k in which], bw,
        )

    away = grads((0, 1), 1 - x)
    away, gh_sib, ye2s, act, yf1, grad_hidden = bar((away, gh_sib, ye2s, act, yf1, grad_hidden))

    came, gh_other = go_x(away), go_y(grad_hidden)
    away = grads((2, 3), 1 - x)
    home = grads((0, 1, 2, 3), x)
    yb1s, yb2s = go_c(yb1), go_c(yb2)
    grad_f = grad_pre.astype(F32)
    terms = []
    for index, (da, db) in enumerate(OFFSETS):
        terms.append(
            jnp.sum(grad_f * padded[1 + da : 1 + da + grid_rows, 1 + db : 1 + db + GW], axis=(0, 1))
        )
    terms = jnp.stack(terms + [jnp.sum(grad_f, axis=(0, 1))])
    came, gh_other, yf2, away, home, yb1s, yb2s, act, terms = bar(
        (came, gh_other, yf2, away, home, yb1s, yb2s, act, terms)
    )

    add = lambda p, q: (p.astype(F32) + q.astype(F32)).astype(BF)
    act_other, yf1s = go_y(act), go_c(yf1)
    out0, out1 = go_z(add(home[0], came[0]), order[0]), go_z(add(home[1], came[1]), order[1])
    came = go_x(away)
    from_a = {0: (a0, a0s), 1: (a1, a1s), 2: (a2, a2s), 3: (a3, a3s)}
    from_e = {0: (e0, e0s), 1: (e1, e1s), 2: (e2, e2s), 3: (e3, e3s)}
    from_b = {0: (b0, b0s), 1: (b1, b1s), 2: (b2, b2s), 3: (b3, b3s)}
    from_f = {0: (f0, f0s), 1: (f1, f1s), 2: (f2, f2s), 3: (f3, f3s)}
    grad_w_in = weight_grad(
        c,
        [
            (l1 * NX + x, k1, from_a, (ya1, ya1s)),
            (l2 * NX + x, k2, from_a, (ya2, ya2s)),
            (l1 * NX + 1 - x, k1, from_e, (ye1, ye1s)),
            (l2 * NX + 1 - x, k2, from_e, (ye2, ye2s)),
        ],
        grad_hidden, gh_other, True, blocks,
    )
    out0, out1, came, act_other, yf1s, grad_w_in = bar((out0, out1, came, act_other, yf1s, grad_w_in))

    out2, yf2s, terms_other = go_z(add(home[2], came[0]), order[2]), go_c(yf2), go_y(terms)
    grad_w_out = weight_grad(
        c,
        [
            (l1 * NX + x, k1, from_b, (yb1, yb1s)),
            (l2 * NX + x, k2, from_b, (yb2, yb2s)),
            (l1 * NX + 1 - x, k1, from_f, (yf1, yf1s)),
            (l2 * NX + 1 - x, k2, from_f, (yf2, yf2s)),
        ],
        act, act_other, False, blocks,
    )
    total = home[3].astype(F32) + came[1].astype(F32) + out0.astype(F32) + out1.astype(F32) + out2.astype(F32)
    grad_tokens = total.astype(BF)

    terms = terms + terms_other
    return (grad_tokens, grad_w_in, grad_w_out, terms[:9], terms[9])


def solution(mesh):
    split = mesh.shape["space"] == 2 and mesh.shape["tensor"] == NZ * NX * NC
    return jax.shard_map(
        shards if split else shards_any,
        mesh=mesh,
        in_specs=(
            P("space", "tensor"),
            P("space", "tensor"),
            P(None, "tensor"),
            P("tensor", None),
            P(None, "tensor"),
            P("tensor"),
        ),
        out_specs=(
            P("space", "tensor"),
            P("space", "tensor"),
            P("tensor", "space"),
            P(None, "tensor"),
            P("tensor"),
        ),
        check_vma=False,
    )
```

time: 282 us -> 186 us (0.66)
  waiting for transfers between devices: 121 us -> 52.9 us
  local copies, waits for them, and re-layouts: 60.6 us -> 9.62 us
  Pallas kernels: 55.8 us -> 66.8 us
  starting transfers between devices: 31.8 us -> 37.8 us
  other arithmetic: 10.5 us -> 15.4 us
    dynamic_slice x4 -> x0, local copies, waits for them, and re-layouts: 37.2 us -> none  [the longest x1 31.8 us: shards(): lax.dynamic_index_in_dim(w_out.reshape(ff, NZ * NX, NC, bw), 1 - c, 2, ke...]
    ppermute x7 -> x12, waiting for transfers between devices: 53.8 us -> 18.6 us  [go_y(): return lax.ppermute(v, 'space', [(0, 1), (1, 0)])]
    ppermute x10, waiting for transfers between devices: 53.3 us -> 26 us  [go_z(): lax.ppermute(v, 'tensor', [(dev(z, x, c), dev((z + k) % NZ, x, c)) for z,...]
    reshape x1 -> x2, local copies, waits for them, and re-layouts: 15.2 us -> 0.07 us  [the longest x1 0.03 us: shards(): jnp.where(first, hidden[grid_rows - 1:], hidden[:1])]
    pallas_call x0 -> x1, Pallas kernels: none -> 6.87 us  [pack(): pl.pallas_call(body, grid_spec=pltpu.PrefetchScalarGridSpec(num_scalar_pr...]
    select_n x2 -> x8, other arithmetic: 0.03 us -> 6.6 us  [the longest x6 6.58 us: pick(): value = jnp.where(j == key, array, value)]
    ppermute x11 -> x9, waiting for transfers between devices: 14.2 us -> 8.2 us  [go_x(): lax.ppermute(v, 'tensor', [(dev(z, x, c), dev(z, 1 - x, c)) for z, x, c i...]
    ppermute x7 -> x12, starting transfers between devices: 9 us -> 13.5 us  [go_y(): return lax.ppermute(v, 'space', [(0, 1), (1, 0)])]
  transfers between devices with their start and end apart: 35 -> 57, of which waited for: 16 -> 15; matrix products, arithmetic and copies ran while one was open for 23% -> 8% of each run, Pallas kernels for 20% -> 36%
where the time goes in v2:
time: 186 us; the launch traced here: 185 us
  Pallas kernels  66.8 us (36%)
  waiting for transfers between devices  52.9 us (28%)
  starting transfers between devices  37.8 us (20%)
  other arithmetic  15.4 us (8%)
  local copies, waits for them, and re-layouts  9.62 us (5%)
  between operations  2.04 us (1%)
    ppermute x10, waiting for transfers between devices, go_z(): lax.ppermute(v, 'tensor', [(dev(z, x, c), dev((z + k) % NZ, x, c)) for z,...  26 us
    pallas_call x2, Pallas kernels, weight_grad(): pl.pallas_call(body, grid_spec=pltpu.PrefetchScalarGridSpec(num_scalar_pr...  23.9 us
    pallas_call x4, Pallas kernels, project(): pl.pallas_call(body, grid_spec=pltpu.PrefetchScalarGridSpec(num_scalar_pr...  22.1 us
    ppermute x12, waiting for transfers between devices, go_y(): return lax.ppermute(v, 'space', [(0, 1), (1, 0)])  18.6 us
    pallas_call x3, Pallas kernels, token_grads(): pl.pallas_call(body, grid_spec=pltpu.PrefetchScalarGridSpec(num_scalar_pr...  13.9 us
    ppermute x12, starting transfers between devices, go_y(): return lax.ppermute(v, 'space', [(0, 1), (1, 0)])  13.5 us
    ppermute x9, starting transfers between devices, go_x(): lax.ppermute(v, 'tensor', [(dev(z, x, c), dev(z, 1 - x, c)) for z, x, c i...  10.6 us
    ppermute x10, starting transfers between devices, go_z(): lax.ppermute(v, 'tensor', [(dev(z, x, c), dev((z + k) % NZ, x, c)) for z,...  8.87 us
  transfers between devices with their start and end apart: 57, of which 15 were waited for; matrix products, arithmetic and copies ran while one was open for 8% of the time, Pallas kernels for 36%

profile of v2, /device:TPU:0, one launch (start us, length us, event | category | flops | bytes accessed | tf_op | source)
XLA Modules:
  0.0 184.5 jit_solution(14021373942652375375)
XLA Ops:
  0.6 3.1 %collective-permute-start = (bf16[392,384]{1,0:T(8,128)(2,1)}, bf16[392,384]{1,0:T(8,128)(2,1)S(1)}, u32[]{:S(2)}, u32[]{:S(2)}) collective-permute-start(bf16[392,384]{1,0:T(8,128)(2,1)} %refs_10_.3), channel_id=1, source_target_pairs={{0,4},{1,5},{2,6},{3,7},{4,8},{5,9},{6,10},{7,11},{8,12},{9,13},{1... | collective-permute-start | bytes 903176 | tf_op jit(solution)/shard_map/ppermute | solution.py:94
  3.7 1.5 collective-permute-start.1
  5.2 6.9 %pack.1 = bf16[3072,768]{1,0:T(8,128)(2,1)} custom-call(s32[1]{0:T(128)} %bitcast.4.core_ref, bf16[6144,768]{1,0:T(8,128)(2,1)} %wo.5), custom_call_target="tpu_custom_call" | custom-call | bytes 9437184 | tf_op jit(solution)/shard_map/pack/pallas_call | solution.py:217
  12.1 1.0 collective-permute-done.refs_4_.refs_2_.refs_12_
  13.2 1.1 collective-permute-start.3
  14.3 1.5 collective-permute-start.4
  16.2 8.3 %collective-permute-done.3.refs_0_.refs_4_.refs_14_ = bf16[392,384]{1,0:T(8,128)(2,1)S(1)} collective-permute-done((bf16[392,384]{1,0:T(8,128)(2,1)S(1)}, bf16[392,384]{1,0:T(8,128)(2,1)S(1)}, u32[]{:S(2)}, u32[]{:S(2)}) %collective-permute-start.3) | collective-permute-done | bytes 301088 | tf_op jit(solution)/shard_map/ppermute | solution.py:94
  25.5 1.5 collective-permute-start.12
  27.7 1.5 collective-permute-start.9
  29.2 4.4 %project.4.refs_11_ = f32[392,768]{1,0:T(8,128)S(1)} custom-call(s32[4]{0:T(128)S(1)} %pad_add_fusion.1.index_ref, bf16[392,384]{1,0:T(8,128)(2,1)S(1)} %copy-done.9, bf16[392,384]{1,0:T(8,128)(2,1)S(1)} %collective-permute-done.2.refs_1_.refs_11_, bf16[392,384]{1,0:T(8,128)(2,1)S(1)} %collective-permute-done.1.refs_2_.refs_20_.refs_30_, ...), custom_call_target="tpu_custom_call" | custom-call | flops 1387266048 | bytes 5947392 | tf_op jit(solution)/shard_map/project/pallas_call | solution.py:151
  33.7 1.6 collective-permute-done.12.refs_8_
  35.3 3.1 %collective-permute-done.8.refs_4_.refs_6_.refs_16_ = bf16[392,384]{1,0:T(8,128)(2,1)S(1)} collective-permute-done((bf16[392,384]{1,0:T(8,128)(2,1)S(1)}, bf16[392,384]{1,0:T(8,128)(2,1)S(1)}, u32[]{:S(2)}, u32[]{:S(2)}) %collective-permute-start.8) | collective-permute-done | bytes 301088 | tf_op jit(solution)/shard_map/ppermute | solution.py:94
  39.7 1.5 collective-permute-start.14
  41.8 6.3 %collective-permute-done.17.refs_28_ = bf16[392,384]{1,0:T(8,128)(2,1)} collective-permute-done((bf16[392,384]{1,0:T(8,128)(2,1)}, bf16[392,384]{1,0:T(8,128)(2,1)}, u32[]{:S(2)}, u32[]{:S(2)}) %collective-permute-start.17) | collective-permute-done | bytes 301088 | tf_op jit(solution)/shard_map/ppermute | solution.py:106
  48.1 1.7 collective-permute-done.13.refs_2_.refs_12_
  50.0 1.6 collective-permute-start.21
  51.6 1.5 collective-permute-start.19
  54.0 6.5 %project.5 = bf16[392,768]{1,0:T(8,128)(2,1)S(1)} custom-call(s32[6]{0:T(128)S(1)} %stack.186.index_ref, bf16[392,384]{1,0:T(8,128)(2,1)S(1)} %collective-permute-done.3.refs_0_.refs_4_.refs_14_, bf16[392,384]{1,0:T(8,128)(2,1)S(1)} %copy-done.40, bf16[392,384]{1,0:T(8,128)(2,1)S(1)} %collective-permute-done.4.refs_2_.refs_22_.refs_32_, ...), custom_call_target="tpu_custom_call" | custom-call | flops 2312110080 | bytes 8306688 | tf_op jit(solution)/shard_map/project/pallas_call | solution.py:151
  60.5 4.0 %collective-permute-done.18.refs_6_.refs_4_.refs_14_ = bf16[392,384]{1,0:T(8,128)(2,1)} collective-permute-done((bf16[392,384]{1,0:T(8,128)(2,1)S(1)}, bf16[392,384]{1,0:T(8,128)(2,1)}, u32[]{:S(2)}, u32[]{:S(2)}) %collective-permute-start.18) | collective-permute-done | bytes 301088 | tf_op jit(solution)/shard_map/ppermute | solution.py:94
  65.4 1.0 pad_maximum_fusion
  68.1 7.4 %collective-permute-done.24.refs_2_.refs_22_.refs_32_ = bf16[392,384]{1,0:T(8,128)(2,1)S(1)} collective-permute-done((bf16[392,384]{1,0:T(8,128)(2,1)S(1)}, bf16[392,384]{1,0:T(8,128)(2,1)S(1)}, u32[]{:S(2)}, u32[]{:S(2)}) %collective-permute-start.24) | collective-permute-done | bytes 301088 | tf_op jit(solution)/shard_map/ppermute | solution.py:98
  75.5 3.6 %collective-permute-done.23.refs_0_.refs_6_.refs_16_ = bf16[392,384]{1,0:T(8,128)(2,1)S(1)} collective-permute-done((bf16[392,384]{1,0:T(8,128)(2,1)}, bf16[392,384]{1,0:T(8,128)(2,1)S(1)}, u32[]{:S(2)}, u32[]{:S(2)}) %collective-permute-start.23) | collective-permute-done | bytes 301088 | tf_op jit(solution)/shard_map/ppermute | solution.py:94
  79.1 2.1 %select_select_fusion.2 = (bf16[392,384]{1,0:T(8,128)(2,1)}, bf16[392,384]{1,0:T(8,128)(2,1)}) fusion(bf16[392,384]{1,0:T(8,128)(2,1)} %collective-permute-done.18.refs_6_.refs_4_.refs_14_, bf16[392,384]{1,0:T(8,128)(2,1)S(1)} %collective-permute-done.13.refs_2_.refs_12_, bf16[392,384]{1,0:T(8,128)(2,1)S(1)} %collective-permute-done.23.refs_0_.refs_6_.refs_16_, ...), kind=kLoop, calls=%fused_computation.71 | loop fusion | flops 602112 | bytes 1806340 | tf_op jit(solution)/shard_map/jit(_where)/select_n | solution.py:336
  81.3 1.5 collective-permute-start.32
  82.8 1.5 collective-permute-start.29
  84.5 1.7 slice.154.refs_38_
  87.8 1.0 copy-done.47
  88.7 1.0 copy-done.52
  90.7 5.7 %project.6.refs_9_ = f32[392,768]{1,0:T(8,128)S(1)} custom-call(s32[5]{0:T(128)S(1)} %stack.187.index_ref, bf16[392,384]{1,0:T(8,128)(2,1)S(1)} %copy-done.11, bf16[392,384]{1,0:T(8,128)(2,1)S(1)} %copy-done.47, bf16[392,384]{1,0:T(8,128)(2,1)S(1)} %collective-permute-done.13.refs_2_.refs_12_, bf16[392,384]{1,0:T(8,128)(2,1)S(1)} %copy-done.52, ...), custom_call_target="tpu_custom_call" | custom-call | flops 1849688064 | bytes 7127040 | tf_op jit(solution)/shard_map/project/pallas_call | solution.py:151
  98.4 2.1 %multiply_convert_fusion = (bf16[7,56,768]{2,1,0:T(8,128)(2,1)}, f32[7,56,768]{2,1,0:T(8,128)S(1)}) fusion(f32[9,58,768]{2,1,0:T(8,128)S(1)} %fusion.30, f32[768]{0:T(1024)S(1)} %get-tuple-element.169, f32[768]{0:T(1024)S(1)} %get-tuple-element.170, f32[768]{0:T(1024)S(1)} %get-tuple-element.163, f32[768]{0:T(1024)S(1)} %get-tuple-element.164, ...), kind=kLoop, calls=%fused_computation.47 | loop fusion | flops 8128512 | bytes 12675072 | tf_op jit(solution)/shard_map/convert_element_type | solution.py:420
  101.9 5.4 %project.7 = bf16[392,768]{1,0:T(8,128)(2,1)S(1)} custom-call(s32[5]{0:T(128)S(1)} %stack.180.index_ref, bf16[392,384]{1,0:T(8,128)(2,1)S(1)} %collective-permute-done.23.refs_0_.refs_6_.refs_16_, bf16[392,384]{1,0:T(8,128)(2,1)} %collective-permute-done.31.refs_1_.refs_7_.refs_17_, bf16[392,384]{1,0:T(8,128)(2,1)S(1)} %collective-permute-done.24.refs_2_.refs_22_.refs_32_, ...), custom_call_target="tpu_custom_call" | custom-call | flops 1849688064 | bytes 7127040 | tf_op jit(solution)/shard_map/project/pallas_call | solution.py:151
  107.5 1.6 collective-permute-start.38
  109.1 3.1 %collective-permute-done.38 = bf16[1,56,768]{2,1,0:T(8,128)(2,1)S(1)} collective-permute-done((bf16[1,56,768]{2,1,0:T(8,128)(2,1)S(1)}, bf16[1,56,768]{2,1,0:T(8,128)(2,1)S(1)}, u32[]{:S(2)}, u32[]{:S(2)}) %collective-permute-start.38) | collective-permute-done | bytes 86048 | tf_op jit(solution)/shard_map/ppermute | solution.py:106
  113.7 1.9 %select_select_fusion = (bf16[392,384]{1,0:T(8,128)(2,1)}, bf16[392,384]{1,0:T(8,128)(2,1)S(1)}) fusion(bf16[392,384]{1,0:T(8,128)(2,1)} %copy-done.3, bf16[392,384]{1,0:T(8,128)(2,1)S(1)} %collective-permute-done.24.refs_2_.refs_22_.refs_32_, bf16[392,384]{1,0:T(8,128)(2,1)} %copy-done.6, pred[]{:T(512)S(6)} %eq.66, pred[]{:T(512)S(6)} %eq.65, ...), kind=kLoop, calls=%fused_computation.69 | loop fusion | flops 602112 | bytes 1806340 | tf_op jit(solution)/shard_map/jit(_where)/select_n | solution.py:336
  115.6 1.6 collective-permute-start.43
  118.0 4.2 %token_grads.3 = bf16[2,392,384]{2,1,0:T(8,128)(2,1)} custom-call(s32[4]{0:T(128)S(1)} %pad_add_fusion.index_ref, bf16[392,768]{1,0:T(8,128)(2,1)S(1)} %bitcast.52, bf16[392,768]{1,0:T(8,128)(2,1)S(1)} %collective-permute-done.41.gs, bf16[6144,768]{1,0:T(8,128)(2,1)} %wo.5, bf16[3072,768]{1,0:T(8,128)(2,1)} %collective-permute-done.7.ws), custom_call_target="tpu_custom_call" | custom-call | flops 924844032 | bytes 2961408 | tf_op jit(solution)/shard_map/token_grads/pallas_call | solution.py:182
  122.3 3.3 %collective-permute-done.43.refs_28_ = bf16[392,384]{1,0:T(8,128)(2,1)S(1)} collective-permute-done((bf16[392,384]{1,0:T(8,128)(2,1)S(1)}, bf16[392,384]{1,0:T(8,128)(2,1)S(1)}, u32[]{:S(2)}, u32[]{:S(2)}) %collective-permute-start.43) | collective-permute-done | bytes 301088 | tf_op jit(solution)/shard_map/ppermute | solution.py:106
  126.2 1.6 collective-permute-start.45
  127.8 1.0 fusion.14
  129.2 3.7 %token_grads.4 = bf16[2,392,384]{2,1,0:T(8,128)(2,1)S(1)} custom-call(s32[4]{0:T(128)S(1)} %pad_add_fusion.2.index_ref, bf16[392,768]{1,0:T(8,128)(2,1)S(1)} %bitcast.54, bf16[392,768]{1,0:T(8,128)(2,1)S(1)} %collective-permute-done.41.gs, bf16[6144,768]{1,0:T(8,128)(2,1)} %wo.5, bf16[3072,768]{1,0:T(8,128)(2,1)} %collective-permute-done.7.ws), custom_call_target="tpu_custom_call" | custom-call | flops 924844032 | bytes 2961408 | tf_op jit(solution)/shard_map/token_grads/pallas_call | solution.py:182
  133.1 6.0 %token_grads.5 = bf16[4,392,384]{2,1,0:T(8,128)(2,1)S(1)} custom-call(s32[8]{0:T(128)S(1)} %stack.199.index_ref, bf16[392,768]{1,0:T(8,128)(2,1)S(1)} %bitcast.55, bf16[392,768]{1,0:T(8,128)(2,1)S(1)} %collective-permute-done.41.gs, bf16[6144,768]{1,0:T(8,128)(2,1)} %wo.5, bf16[3072,768]{1,0:T(8,128)(2,1)} %collective-permute-done.7.ws), custom_call_target="tpu_custom_call" | custom-call | flops 1849688064 | bytes 5922816 | tf_op jit(solution)/shard_map/token_grads/pallas_call | solution.py:182
  140.4 4.0 %collective-permute-done.45.r = bf16[392,768]{1,0:T(8,128)(2,1)} collective-permute-done((bf16[392,768]{1,0:T(8,128)(2,1)S(1)}, bf16[392,768]{1,0:T(8,128)(2,1)}, u32[]{:S(2)}, u32[]{:S(2)}) %collective-permute-start.45) | collective-permute-done | bytes 602144 | tf_op jit(solution)/shard_map/ppermute | solution.py:106
  144.5 1.6 collective-permute-start.56
  147.0 1.2 fusion.35
  148.9 3.8 %collective-permute-start.50 = (bf16[392,384]{1,0:T(8,128)(2,1)S(1)}, bf16[392,384]{1,0:T(8,128)(2,1)S(1)}, u32[]{:S(2)}, u32[]{:S(2)}) collective-permute-start(bf16[392,384]{1,0:T(8,128)(2,1)S(1)} %get-tuple-element.173), channel_id=1, source_target_pairs={{0,4},{1,5},{2,6},{3,7},{4,8},{5,9},{6,10},{7,11},{8,12},{9,13},{1... | collective-permute-start | bytes 903176 | tf_op jit(solution)/shard_map/ppermute | solution.py:94
  152.9 11.8 %weight_grad.2 = bf16[3072,768]{1,0:T(8,128)(2,1)} custom-call(s32[9]{0:T(128)S(1)} %stack.217.index_ref, bf16[392,768]{1,0:T(8,128)(2,1)} %bitcast.56, bf16[392,768]{1,0:T(8,128)(2,1)} %collective-permute-done.45.r, bf16[392,384]{1,0:T(8,128)(2,1)S(1)} %copy-done.10, bf16[392,384]{1,0:T(8,128)(2,1)S(1)} %copy-done.34, ...), custom_call_target="tpu_custom_call" | custom-call | flops 3699376128 | bytes 9535488 | tf_op jit(solution)/shard_map/weight_grad/pallas_call | solution.py:301
  165.6 4.3 %collective-permute-done.49 = bf16[392,384]{1,0:T(8,128)(2,1)S(1)} collective-permute-done((bf16[392,384]{1,0:T(8,128)(2,1)S(1)}, bf16[392,384]{1,0:T(8,128)(2,1)S(1)}, u32[]{:S(2)}, u32[]{:S(2)}) %collective-permute-start.49) | collective-permute-done | bytes 301088 | tf_op jit(solution)/shard_map/ppermute | solution.py:94
  171.5 12.1 %weight_grad.3 = bf16[768,3072]{1,0:T(8,128)(2,1)} custom-call(s32[9]{0:T(128)S(1)} %stack.217.index_ref, bf16[392,768]{1,0:T(8,128)(2,1)} %bitcast.61, bf16[392,768]{1,0:T(8,128)(2,1)} %copy-done.68, bf16[392,384]{1,0:T(8,128)(2,1)S(1)} %copy-done.12, bf16[392,384]{1,0:T(8,128)(2,1)S(1)} %copy-done.48, bf16[392,384]{1,0:T(8,128)(2,1)S(1)} %copy-done.18, ...), custom_call_target="tpu_custom_call" | custom-call | flops 3699376128 | bytes 9535488 | tf_op jit(solution)/shard_map/weight_grad/pallas_call | solution.py:301
  (281 shorter events, 23.1 us)
Async XLA Ops:
  0.6 12.5 %collective-permute-start = (bf16[392,384]{1,0:T(8,128)(2,1)}, bf16[392,384]{1,0:T(8,128)(2,1)S(1)}, u32[]{:S(2)}, u32[]{:S(2)}) collective-permute-start(bf16[392,384]{1,0:T(8,128)(2,1)} %refs_10_.3), channel_id=1, source_target_pairs={{0,4},{1,5},{2,6},{3,7},{4,8},{5,9},{6,10},{7,11},{8,12},{9,13},{1... | collective-permute-start | bytes 903176 | tf_op jit(solution)/shard_map/ppermute | solution.py:94
  3.7 9.4 %collective-permute-start.1 = (bf16[392,384]{1,0:T(8,128)(2,1)}, bf16[392,384]{1,0:T(8,128)(2,1)S(1)}, u32[]{:S(2)}, u32[]{:S(2)}) collective-permute-start(bf16[392,384]{1,0:T(8,128)(2,1)} %refs_10_.3), channel_id=1, source_target_pairs={{0,2},{1,3},{2,0},{3,1},{4,6},{5,7},{6,4},{7,5},{8,10},{9,11},{10,... | collective-permute-start | bytes 903176 | tf_op jit(solution)/shard_map/ppermute | solution.py:98
  5.2 7.9 %collective-permute-start.2 = (bf16[392,384]{1,0:T(8,128)(2,1)}, bf16[392,384]{1,0:T(8,128)(2,1)S(1)}, u32[]{:S(2)}, u32[]{:S(2)}) collective-permute-start(bf16[392,384]{1,0:T(8,128)(2,1)} %refs_10_.3), channel_id=1, source_target_pairs={{0,1},{1,0},{2,3},{3,2},{4,5},{5,4},{6,7},{7,6},{8,9},{9,8},{10,11... | collective-permute-start | bytes 903176 | tf_op jit(solution)/shard_map/ppermute | solution.py:102
  13.1 11.5 %collective-permute-start.7 = (bf16[3072,768]{1,0:T(8,128)(2,1)}, bf16[3072,768]{1,0:T(8,128)(2,1)}, u32[]{:S(2)}, u32[]{:S(2)}) collective-permute-start(bf16[3072,768]{1,0:T(8,128)(2,1)} %pack.1), channel_id=1, source_target_pairs={{0,1},{1,0},{2,3},{3,2},{4,5},{5,4},{6,7},{7,6},{8,9},{9,8},{10,11... | collective-permute-start | bytes 14155784 | tf_op jit(solution)/shard_map/ppermute | solution.py:102
  13.2 11.3 %collective-permute-start.3 = (bf16[392,384]{1,0:T(8,128)(2,1)S(1)}, bf16[392,384]{1,0:T(8,128)(2,1)S(1)}, u32[]{:S(2)}, u32[]{:S(2)}) collective-permute-start(bf16[392,384]{1,0:T(8,128)(2,1)S(1)} %collective-permute-done.refs_4_.refs_2_.refs_12_), channel_id=1, source_target_pairs={{0,4},{1,5},{2,6},{3,7},{4,8},{5,9},{6,10},{7,11},{8,12},{9,13},{1... | collective-permute-start | bytes 903176 | tf_op jit(solution)/shard_map/ppermute | solution.py:94
  14.3 10.3 %collective-permute-start.4 = (bf16[392,384]{1,0:T(8,128)(2,1)S(1)}, bf16[392,384]{1,0:T(8,128)(2,1)S(1)}, u32[]{:S(2)}, u32[]{:S(2)}) collective-permute-start(bf16[392,384]{1,0:T(8,128)(2,1)S(1)} %collective-permute-done.refs_4_.refs_2_.refs_12_), channel_id=1, source_target_pairs={{0,2},{1,3},{2,0},{3,1},{4,6},{5,7},{6,4},{7,5},{8,10},{9,11},{10,... | collective-permute-start | bytes 903176 | tf_op jit(solution)/shard_map/ppermute | solution.py:98
  15.7 8.8 %collective-permute-start.5 = (bf16[392,384]{1,0:T(8,128)(2,1)S(1)}, bf16[392,384]{1,0:T(8,128)(2,1)S(1)}, u32[]{:S(2)}, u32[]{:S(2)}) collective-permute-start(bf16[392,384]{1,0:T(8,128)(2,1)S(1)} %collective-permute-done.refs_4_.refs_2_.refs_12_), channel_id=1, source_target_pairs={{0,1},{1,0},{2,3},{3,2},{4,5},{5,4},{6,7},{7,6},{8,9},{9,8},{10,11... | collective-permute-start | bytes 903176 | tf_op jit(solution)/shard_map/ppermute | solution.py:102
  15.7 8.8 %collective-permute-start.6 = (bf16[392,384]{1,0:T(8,128)(2,1)S(1)}, bf16[392,384]{1,0:T(8,128)(2,1)S(1)}, u32[]{:S(2)}, u32[]{:S(2)}) collective-permute-start(bf16[392,384]{1,0:T(8,128)(2,1)S(1)} %collective-permute-done.1.refs_2_.refs_20_.refs_30_), channel_id=1, source_target_pairs={{0,1},{1,0},{2,3},{3,2},{4,5},{5,4},{6,7},{7,6},{8,9},{9,8},{10,11... | collective-permute-start | bytes 903176 | tf_op jit(solution)/shard_map/ppermute | solution.py:102
  24.6 10.7 %collective-permute-start.10 = (bf16[392,384]{1,0:T(8,128)(2,1)S(1)}, bf16[392,384]{1,0:T(8,128)(2,1)S(1)}, u32[]{:S(2)}, u32[]{:S(2)}) collective-permute-start(bf16[392,384]{1,0:T(8,128)(2,1)S(1)} %collective-permute-done.3.refs_0_.refs_4_.refs_14_), channel_id=1, source_target_pairs={{0,1},{1,0},{2,3},{3,2},{4,5},{5,4},{6,7},{7,6},{8,9},{9,8},{10,11... | collective-permute-start | bytes 903176 | tf_op jit(solution)/shard_map/ppermute | solution.py:102
  25.5 9.8 %collective-permute-start.12 = (bf16[392,384]{1,0:T(8,128)(2,1)}, bf16[392,384]{1,0:T(8,128)(2,1)}, u32[]{:S(2)}, u32[]{:S(2)}) collective-permute-start(bf16[392,384]{1,0:T(8,128)(2,1)} %select_select_fusion.7), channel_id=1, source_target_pairs={{0,16},{16,0},{1,17},{17,1},{2,18},{18,2},{3,19},{19,3},{4,20},{20... | collective-permute-start | bytes 903176 | tf_op jit(solution)/shard_map/ppermute | solution.py:106
  27.0 8.3 %collective-permute-start.11 = (bf16[392,384]{1,0:T(8,128)(2,1)S(1)}, bf16[392,384]{1,0:T(8,128)(2,1)}, u32[]{:S(2)}, u32[]{:S(2)}) collective-permute-start(bf16[392,384]{1,0:T(8,128)(2,1)S(1)} %collective-permute-done.4.refs_2_.refs_22_.refs_32_), channel_id=1, source_target_pairs={{0,1},{1,0},{2,3},{3,2},{4,5},{5,4},{6,7},{7,6},{8,9},{9,8},{10,11... | collective-permute-start | bytes 903176 | tf_op jit(solution)/shard_map/ppermute | solution.py:102
  27.2 11.2 %collective-permute-start.8 = (bf16[392,384]{1,0:T(8,128)(2,1)S(1)}, bf16[392,384]{1,0:T(8,128)(2,1)S(1)}, u32[]{:S(2)}, u32[]{:S(2)}) collective-permute-start(bf16[392,384]{1,0:T(8,128)(2,1)S(1)} %collective-permute-done.3.refs_0_.refs_4_.refs_14_), channel_id=1, source_target_pairs={{0,4},{1,5},{2,6},{3,7},{4,8},{5,9},{6,10},{7,11},{8,12},{9,13},{1... | collective-permute-start | bytes 903176 | tf_op jit(solution)/shard_map/ppermute | solution.py:94
  27.7 10.7 %collective-permute-start.9 = (bf16[392,384]{1,0:T(8,128)(2,1)S(1)}, bf16[392,384]{1,0:T(8,128)(2,1)S(1)}, u32[]{:S(2)}, u32[]{:S(2)}) collective-permute-start(bf16[392,384]{1,0:T(8,128)(2,1)S(1)} %collective-permute-done.3.refs_0_.refs_4_.refs_14_), channel_id=1, source_target_pairs={{0,2},{1,3},{2,0},{3,1},{4,6},{5,7},{6,4},{7,5},{8,10},{9,11},{10,... | collective-permute-start | bytes 903176 | tf_op jit(solution)/shard_map/ppermute | solution.py:98
  39.2 8.9 %collective-permute-start.17 = (bf16[392,384]{1,0:T(8,128)(2,1)}, bf16[392,384]{1,0:T(8,128)(2,1)}, u32[]{:S(2)}, u32[]{:S(2)}) collective-permute-start(bf16[392,384]{1,0:T(8,128)(2,1)} %select_select_fusion.6), channel_id=1, source_target_pairs={{0,16},{16,0},{1,17},{17,1},{2,18},{18,2},{3,19},{19,3},{4,20},{20... | collective-permute-start | bytes 903176 | tf_op jit(solution)/shard_map/ppermute | solution.py:106
  39.7 10.1 %collective-permute-start.13 = (bf16[392,384]{1,0:T(8,128)(2,1)S(1)}, bf16[392,384]{1,0:T(8,128)(2,1)S(1)}, u32[]{:S(2)}, u32[]{:S(2)}) collective-permute-start(bf16[392,384]{1,0:T(8,128)(2,1)S(1)} %copy-done.11), channel_id=1, source_target_pairs={{0,4},{1,5},{2,6},{3,7},{4,8},{5,9},{6,10},{7,11},{8,12},{9,13},{1... | collective-permute-start | bytes 903176 | tf_op jit(solution)/shard_map/ppermute | solution.py:94
  39.7 10.1 %collective-permute-start.14 = (bf16[392,384]{1,0:T(8,128)(2,1)S(1)}, bf16[392,384]{1,0:T(8,128)(2,1)S(1)}, u32[]{:S(2)}, u32[]{:S(2)}) collective-permute-start(bf16[392,384]{1,0:T(8,128)(2,1)S(1)} %collective-permute-done.8.refs_4_.refs_6_.refs_16_), channel_id=1, source_target_pairs={{0,2},{1,3},{2,0},{3,1},{4,6},{5,7},{6,4},{7,5},{8,10},{9,11},{10,... | collective-permute-start | bytes 903176 | tf_op jit(solution)/shard_map/ppermute | solution.py:98
  41.2 8.6 %collective-permute-start.15 = (bf16[392,384]{1,0:T(8,128)(2,1)S(1)}, bf16[392,384]{1,0:T(8,128)(2,1)S(1)}, u32[]{:S(2)}, u32[]{:S(2)}) collective-permute-start(bf16[392,384]{1,0:T(8,128)(2,1)S(1)} %collective-permute-done.8.refs_4_.refs_6_.refs_16_), channel_id=1, source_target_pairs={{0,1},{1,0},{2,3},{3,2},{4,5},{5,4},{6,7},{7,6},{8,9},{9,8},{10,11... | collective-permute-start | bytes 903176 | tf_op jit(solution)/shard_map/ppermute | solution.py:102
  41.2 8.6 %collective-permute-start.16 = (bf16[392,384]{1,0:T(8,128)(2,1)S(1)}, bf16[392,384]{1,0:T(8,128)(2,1)S(1)}, u32[]{:S(2)}, u32[]{:S(2)}) collective-permute-start(bf16[392,384]{1,0:T(8,128)(2,1)S(1)} %collective-permute-done.9.refs_6_.refs_24_.refs_34_), channel_id=1, source_target_pairs={{0,1},{1,0},{2,3},{3,2},{4,5},{5,4},{6,7},{7,6},{8,9},{9,8},{10,11... | collective-permute-start | bytes 903176 | tf_op jit(solution)/shard_map/ppermute | solution.py:102
  50.0 10.5 %collective-permute-start.21 = (bf16[392,384]{1,0:T(8,128)(2,1)S(1)}, bf16[392,384]{1,0:T(8,128)(2,1)S(1)}, u32[]{:S(2)}, u32[]{:S(2)}) collective-permute-start(bf16[392,384]{1,0:T(8,128)(2,1)S(1)} %select_select_fusion.5), channel_id=1, source_target_pairs={{0,16},{16,0},{1,17},{17,1},{2,18},{18,2},{3,19},{19,3},{4,20},{20... | collective-permute-start | bytes 903176 | tf_op jit(solution)/shard_map/ppermute | solution.py:106
  51.6 13.0 %collective-permute-start.19 = (bf16[392,384]{1,0:T(8,128)(2,1)S(1)}, bf16[392,384]{1,0:T(8,128)(2,1)S(1)}, u32[]{:S(2)}, u32[]{:S(2)}) collective-permute-start(bf16[392,384]{1,0:T(8,128)(2,1)S(1)} %copy-done.11), channel_id=1, source_target_pairs={{0,2},{1,3},{2,0},{3,1},{4,6},{5,7},{6,4},{7,5},{8,10},{9,11},{10,... | collective-permute-start | bytes 903176 | tf_op jit(solution)/shard_map/ppermute | solution.py:98
  53.1 11.5 %collective-permute-start.20 = (bf16[392,384]{1,0:T(8,128)(2,1)S(1)}, bf16[392,384]{1,0:T(8,128)(2,1)S(1)}, u32[]{:S(2)}, u32[]{:S(2)}) collective-permute-start(bf16[392,384]{1,0:T(8,128)(2,1)S(1)} %copy-done.11), channel_id=1, source_target_pairs={{0,1},{1,0},{2,3},{3,2},{4,5},{5,4},{6,7},{7,6},{8,9},{9,8},{10,11... | collective-permute-start | bytes 903176 | tf_op jit(solution)/shard_map/ppermute | solution.py:102
  53.1 11.5 %collective-permute-start.18 = (bf16[392,384]{1,0:T(8,128)(2,1)S(1)}, bf16[392,384]{1,0:T(8,128)(2,1)}, u32[]{:S(2)}, u32[]{:S(2)}) collective-permute-start(bf16[392,384]{1,0:T(8,128)(2,1)S(1)} %collective-permute-done.13.refs_2_.refs_12_), channel_id=1, source_target_pairs={{0,4},{1,5},{2,6},{3,7},{4,8},{5,9},{6,10},{7,11},{8,12},{9,13},{1... | collective-permute-start | bytes 903176 | tf_op jit(solution)/shard_map/ppermute | solution.py:94
  66.4 12.7 %collective-permute-start.27 = (bf16[504,384]{1,0:T(8,128)(2,1)S(1)}, bf16[504,384]{1,0:T(8,128)(2,1)}, u32[]{:S(2)}, u32[]{:S(2)}) collective-permute-start(bf16[504,384]{1,0:T(8,128)(2,1)S(1)} %pad_maximum_fusion), channel_id=1, source_target_pairs={{0,16},{16,0},{1,17},{17,1},{2,18},{18,2},{3,19},{19,3},{4,20},{20... | collective-permute-start | bytes 1161224 | tf_op jit(solution)/shard_map/ppermute | solution.py:106
  67.0 8.5 %collective-permute-start.24 = (bf16[392,384]{1,0:T(8,128)(2,1)S(1)}, bf16[392,384]{1,0:T(8,128)(2,1)S(1)}, u32[]{:S(2)}, u32[]{:S(2)}) collective-permute-start(bf16[392,384]{1,0:T(8,128)(2,1)S(1)} %collective-permute-done.13.refs_2_.refs_12_), channel_id=1, source_target_pairs={{0,2},{1,3},{2,0},{3,1},{4,6},{5,7},{6,4},{7,5},{8,10},{9,11},{10,... | collective-permute-start | bytes 903176 | tf_op jit(solution)/shard_map/ppermute | solution.py:98
  67.5 8.0 %collective-permute-start.25 = (bf16[392,384]{1,0:T(8,128)(2,1)S(1)}, bf16[392,384]{1,0:T(8,128)(2,1)S(1)}, u32[]{:S(2)}, u32[]{:S(2)}) collective-permute-start(bf16[392,384]{1,0:T(8,128)(2,1)S(1)} %collective-permute-done.13.refs_2_.refs_12_), channel_id=1, source_target_pairs={{0,1},{1,0},{2,3},{3,2},{4,5},{5,4},{6,7},{7,6},{8,9},{9,8},{10,11... | collective-permute-start | bytes 903176 | tf_op jit(solution)/shard_map/ppermute | solution.py:102
  67.5 11.6 %collective-permute-start.23 = (bf16[392,384]{1,0:T(8,128)(2,1)}, bf16[392,384]{1,0:T(8,128)(2,1)S(1)}, u32[]{:S(2)}, u32[]{:S(2)}) collective-permute-start(bf16[392,384]{1,0:T(8,128)(2,1)} %collective-permute-done.18.refs_6_.refs_4_.refs_14_), channel_id=1, source_target_pairs={{0,4},{1,5},{2,6},{3,7},{4,8},{5,9},{6,10},{7,11},{8,12},{9,13},{1... | collective-permute-start | bytes 903176 | tf_op jit(solution)/shard_map/ppermute | solution.py:94
  67.6 11.6 %collective-permute-start.26 = (bf16[392,384]{1,0:T(8,128)(2,1)S(1)}, bf16[392,384]{1,0:T(8,128)(2,1)S(1)}, u32[]{:S(2)}, u32[]{:S(2)}) collective-permute-start(bf16[392,384]{1,0:T(8,128)(2,1)S(1)} %collective-permute-done.19.refs_4_.refs_20_.refs_30_), channel_id=1, source_target_pairs={{0,1},{1,0},{2,3},{3,2},{4,5},{5,4},{6,7},{7,6},{8,9},{9,8},{10,11... | collective-permute-start | bytes 903176 | tf_op jit(solution)/shard_map/ppermute | solution.py:102
  75.5 11.7 %collective-permute-start.30 = (bf16[392,384]{1,0:T(8,128)(2,1)}, bf16[392,384]{1,0:T(8,128)(2,1)}, u32[]{:S(2)}, u32[]{:S(2)}) collective-permute-start(bf16[392,384]{1,0:T(8,128)(2,1)} %collective-permute-done.18.refs_6_.refs_4_.refs_14_), channel_id=1, source_target_pairs={{0,1},{1,0},{2,3},{3,2},{4,5},{5,4},{6,7},{7,6},{8,9},{9,8},{10,11... | collective-permute-start | bytes 903176 | tf_op jit(solution)/shard_map/ppermute | solution.py:102
  81.3 15.1 %collective-permute-start.32 = (bf16[392,384]{1,0:T(8,128)(2,1)}, bf16[392,384]{1,0:T(8,128)(2,1)}, u32[]{:S(2)}, u32[]{:S(2)}) collective-permute-start(bf16[392,384]{1,0:T(8,128)(2,1)} %get-tuple-element.178), channel_id=1, source_target_pairs={{0,16},{16,0},{1,17},{17,1},{2,18},{18,2},{3,19},{19,3},{4,20},{20... | collective-permute-start | bytes 903176 | tf_op jit(solution)/shard_map/ppermute | solution.py:106
  82.8 13.7 %collective-permute-start.28 = (bf16[392,384]{1,0:T(8,128)(2,1)S(1)}, bf16[392,384]{1,0:T(8,128)(2,1)S(1)}, u32[]{:S(2)}, u32[]{:S(2)}) collective-permute-start(bf16[392,384]{1,0:T(8,128)(2,1)S(1)} %collective-permute-done.24.refs_2_.refs_22_.refs_32_), channel_id=1, source_target_pairs={{0,4},{1,5},{2,6},{3,7},{4,8},{5,9},{6,10},{7,11},{8,12},{9,13},{1... | collective-permute-start | bytes 903176 | tf_op jit(solution)/shard_map/ppermute | solution.py:94
  82.8 14.3 %collective-permute-start.29 = (bf16[392,384]{1,0:T(8,128)(2,1)S(1)}, bf16[392,384]{1,0:T(8,128)(2,1)S(1)}, u32[]{:S(2)}, u32[]{:S(2)}) collective-permute-start(bf16[392,384]{1,0:T(8,128)(2,1)S(1)} %collective-permute-done.23.refs_0_.refs_6_.refs_16_), channel_id=1, source_target_pairs={{0,2},{1,3},{2,0},{3,1},{4,6},{5,7},{6,4},{7,5},{8,10},{9,11},{10,... | collective-permute-start | bytes 903176 | tf_op jit(solution)/shard_map/ppermute | solution.py:98
  84.3 12.8 %collective-permute-start.31 = (bf16[392,384]{1,0:T(8,128)(2,1)S(1)}, bf16[392,384]{1,0:T(8,128)(2,1)}, u32[]{:S(2)}, u32[]{:S(2)}) collective-permute-start(bf16[392,384]{1,0:T(8,128)(2,1)S(1)} %collective-permute-done.23.refs_0_.refs_6_.refs_16_), channel_id=1, source_target_pairs={{0,1},{1,0},{2,3},{3,2},{4,5},{5,4},{6,7},{7,6},{8,9},{9,8},{10,11... | collective-permute-start | bytes 903176 | tf_op jit(solution)/shard_map/ppermute | solution.py:102
  87.2 20.2 %collective-permute-start.37 = (bf16[392,384]{1,0:T(8,128)(2,1)}, bf16[392,384]{1,0:T(8,128)(2,1)S(1)}, u32[]{:S(2)}, u32[]{:S(2)}) collective-permute-start(bf16[392,384]{1,0:T(8,128)(2,1)} %collective-permute-done.12.refs_8_), channel_id=1, source_target_pairs={{0,1},{1,0},{2,3},{3,2},{4,5},{5,4},{6,7},{7,6},{8,9},{9,8},{10,11... | collective-permute-start | bytes 903176 | tf_op jit(solution)/shard_map/ppermute | solution.py:102
  96.5 10.9 %collective-permute-start.36 = (bf16[392,384]{1,0:T(8,128)(2,1)S(1)}, bf16[392,384]{1,0:T(8,128)(2,1)}, u32[]{:S(2)}, u32[]{:S(2)}) collective-permute-start(bf16[392,384]{1,0:T(8,128)(2,1)S(1)} %copy-done.75), channel_id=1, source_target_pairs={{0,16},{16,0},{1,17},{17,1},{2,18},{18,2},{3,19},{19,3},{4,20},{20... | collective-permute-start | bytes 903176 | tf_op jit(solution)/shard_map/ppermute | solution.py:106
  101.3 7.8 %collective-permute-start.40 = (bf16[392,384]{1,0:T(8,128)(2,1)}, bf16[392,384]{1,0:T(8,128)(2,1)S(1)}, u32[]{:S(2)}, u32[]{:S(2)}) collective-permute-start(bf16[392,384]{1,0:T(8,128)(2,1)} %collective-permute-done.17.refs_28_), channel_id=1, source_target_pairs={{0,1},{1,0},{2,3},{3,2},{4,5},{5,4},{6,7},{7,6},{8,9},{9,8},{10,11... | collective-permute-start | bytes 903176 | tf_op jit(solution)/shard_map/ppermute | solution.py:102
  115.6 10.0 %collective-permute-start.43 = (bf16[392,384]{1,0:T(8,128)(2,1)S(1)}, bf16[392,384]{1,0:T(8,128)(2,1)S(1)}, u32[]{:S(2)}, u32[]{:S(2)}) collective-permute-start(bf16[392,384]{1,0:T(8,128)(2,1)S(1)} %get-tuple-element.176), channel_id=1, source_target_pairs={{0,16},{16,0},{1,17},{17,1},{2,18},{18,2},{3,19},{19,3},{4,20},{20... | collective-permute-start | bytes 903176 | tf_op jit(solution)/shard_map/ppermute | solution.py:106
  117.2 8.3 %collective-permute-start.42 = (bf16[392,384]{1,0:T(8,128)(2,1)S(1)}, bf16[392,384]{1,0:T(8,128)(2,1)S(1)}, u32[]{:S(2)}, u32[]{:S(2)}) collective-permute-start(bf16[392,384]{1,0:T(8,128)(2,1)S(1)} %copy-done.67), channel_id=1, source_target_pairs={{0,1},{1,0},{2,3},{3,2},{4,5},{5,4},{6,7},{7,6},{8,9},{9,8},{10,11... | collective-permute-start | bytes 903176 | tf_op jit(solution)/shard_map/ppermute | solution.py:102
  117.5 21.7 %collective-permute-start.46 = (bf16[392,384]{1,0:T(8,128)(2,1)}, bf16[392,384]{1,0:T(8,128)(2,1)}, u32[]{:S(2)}, u32[]{:S(2)}) collective-permute-start(bf16[392,384]{1,0:T(8,128)(2,1)} %get-tuple-element.175), channel_id=1, source_target_pairs={{0,16},{16,0},{1,17},{17,1},{2,18},{18,2},{3,19},{19,3},{4,20},{20... | collective-permute-start | bytes 903176 | tf_op jit(solution)/shard_map/ppermute | solution.py:106
  117.9 21.8 %collective-permute-start.47 = (bf16[392,384]{1,0:T(8,128)(2,1)}, bf16[392,384]{1,0:T(8,128)(2,1)}, u32[]{:S(2)}, u32[]{:S(2)}) collective-permute-start(bf16[392,384]{1,0:T(8,128)(2,1)} %collective-permute-done.32.refs_8_), channel_id=1, source_target_pairs={{0,1},{1,0},{2,3},{3,2},{4,5},{5,4},{6,7},{7,6},{8,9},{9,8},{10,11... | collective-permute-start | bytes 903176 | tf_op jit(solution)/shard_map/ppermute | solution.py:102
  125.6 14.9 %collective-permute-start.44 = (bf16[2,392,384]{2,1,0:T(8,128)(2,1)}, bf16[2,392,384]{2,1,0:T(8,128)(2,1)}, u32[]{:S(2)}, u32[]{:S(2)}) collective-permute-start(bf16[2,392,384]{2,1,0:T(8,128)(2,1)} %token_grads.3), channel_id=1, source_target_pairs={{0,2},{1,3},{2,0},{3,1},{4,6},{5,7},{6,4},{7,5},{8,10},{9,11},{10,... | collective-permute-start | bytes 1806344 | tf_op jit(solution)/shard_map/ppermute | solution.py:98
  126.2 18.3 %collective-permute-start.45 = (bf16[392,768]{1,0:T(8,128)(2,1)S(1)}, bf16[392,768]{1,0:T(8,128)(2,1)}, u32[]{:S(2)}, u32[]{:S(2)}) collective-permute-start(bf16[392,768]{1,0:T(8,128)(2,1)S(1)} %bitcast.53), channel_id=1, source_target_pairs={{0,16},{16,0},{1,17},{17,1},{2,18},{18,2},{3,19},{19,3},{4,20},{20... | collective-permute-start | bytes 1806344 | tf_op jit(solution)/shard_map/ppermute | solution.py:106
  128.8 10.9 %collective-permute-start.48 = (bf16[392,384]{1,0:T(8,128)(2,1)}, bf16[392,384]{1,0:T(8,128)(2,1)}, u32[]{:S(2)}, u32[]{:S(2)}) collective-permute-start(bf16[392,384]{1,0:T(8,128)(2,1)} %collective-permute-done.36.refs_18_), channel_id=1, source_target_pairs={{0,1},{1,0},{2,3},{3,2},{4,5},{5,4},{6,7},{7,6},{8,9},{9,8},{10,11... | collective-permute-start | bytes 903176 | tf_op jit(solution)/shard_map/ppermute | solution.py:102
  139.1 25.7 %collective-permute-start.53 = (bf16[392,384]{1,0:T(8,128)(2,1)S(1)}, bf16[392,384]{1,0:T(8,128)(2,1)S(1)}, u32[]{:S(2)}, u32[]{:S(2)}) collective-permute-start(bf16[392,384]{1,0:T(8,128)(2,1)S(1)} %copy-done.71), channel_id=1, source_target_pairs={{0,1},{1,0},{2,3},{3,2},{4,5},{5,4},{6,7},{7,6},{8,9},{9,8},{10,11... | collective-permute-start | bytes 903176 | tf_op jit(solution)/shard_map/ppermute | solution.py:102
  146.1 23.8 %collective-permute-start.51 = (bf16[2,392,384]{2,1,0:T(8,128)(2,1)S(1)}, bf16[2,392,384]{2,1,0:T(8,128)(2,1)S(1)}, u32[]{:S(2)}, u32[]{:S(2)}) collective-permute-start(bf16[2,392,384]{2,1,0:T(8,128)(2,1)S(1)} %token_grads.4), channel_id=1, source_target_pairs={{0,2},{1,3},{2,0},{3,1},{4,6},{5,7},{6,4},{7,5},{8,10},{9,11},{10,... | collective-permute-start | bytes 1806344 | tf_op jit(solution)/shard_map/ppermute | solution.py:98
  146.6 23.3 %collective-permute-start.52 = (bf16[392,768]{1,0:T(8,128)(2,1)S(1)}, bf16[392,768]{1,0:T(8,128)(2,1)S(1)}, u32[]{:S(2)}, u32[]{:S(2)}) collective-permute-start(bf16[392,768]{1,0:T(8,128)(2,1)S(1)} %bitcast.62), channel_id=1, source_target_pairs={{0,16},{16,0},{1,17},{17,1},{2,18},{18,2},{3,19},{19,3},{4,20},{20... | collective-permute-start | bytes 1806344 | tf_op jit(solution)/shard_map/ppermute | solution.py:106
  148.3 21.6 %collective-permute-start.49 = (bf16[392,384]{1,0:T(8,128)(2,1)S(1)}, bf16[392,384]{1,0:T(8,128)(2,1)S(1)}, u32[]{:S(2)}, u32[]{:S(2)}) collective-permute-start(bf16[392,384]{1,0:T(8,128)(2,1)S(1)} %get-tuple-element.174), channel_id=1, source_target_pairs={{0,8},{1,9},{2,10},{3,11},{4,12},{5,13},{6,14},{7,15},{8,0},{9,1},... | collective-permute-start | bytes 903176 | tf_op jit(solution)/shard_map/ppermute | solution.py:94
  148.9 20.9 %collective-permute-start.50 = (bf16[392,384]{1,0:T(8,128)(2,1)S(1)}, bf16[392,384]{1,0:T(8,128)(2,1)S(1)}, u32[]{:S(2)}, u32[]{:S(2)}) collective-permute-start(bf16[392,384]{1,0:T(8,128)(2,1)S(1)} %get-tuple-element.173), channel_id=1, source_target_pairs={{0,4},{1,5},{2,6},{3,7},{4,8},{5,9},{6,10},{7,11},{8,12},{9,13},{1... | collective-permute-start | bytes 903176 | tf_op jit(solution)/shard_map/ppermute | solution.py:94
  170.0 13.6 %collective-permute-start.54 = (bf16[392,384]{1,0:T(8,128)(2,1)S(1)}, bf16[392,384]{1,0:T(8,128)(2,1)S(1)}, u32[]{:S(2)}, u32[]{:S(2)}) collective-permute-start(bf16[392,384]{1,0:T(8,128)(2,1)S(1)} %fusion.36), channel_id=1, source_target_pairs={{0,12},{1,13},{2,14},{3,15},{4,0},{5,1},{6,2},{7,3},{8,4},{9,5},{1... | collective-permute-start | bytes 903176 | tf_op jit(solution)/shard_map/ppermute | solution.py:94
  (88 other events, 896.1 us)
